TPU v7x, 32 devices: a whole 2x2x4 slice. The times are simulated.
32 devices in a mesh: rep: 4 (over z), shard: 8 (over y, x, core).
Axes of the slice: x: 2, y: 2, z: 4, core: 2. Of those that a mesh axis runs over, the one named last changes fastest.
Arguments:
- tokens: bfloat16 [8192, 2048], P(('rep', 'shard')), may hold values from -6 to 6
- cotangent: bfloat16 [8192, 2048], P(('rep', 'shard')), may hold values from -6 to 6
- placement_order: int32 [4, 8, 2, 128], P('rep', 'shard'), may hold values from 0 to 127, each once within a row
- seq_lengths: int32 [4, 2, 8], P('rep'), may hold values from 0 to 1024, as said below
- ln_gain: bfloat16 [2048], P('shard'), may hold values from 0.25 to 1.75
- ln_bias: bfloat16 [2048], P('shard'), may hold values from -4 to 4
- qkv_weight: bfloat16 [2048, 6144], P('shard'), may hold values from -0.125 to 0.125
- qkv_bias: bfloat16 [6144], P('shard'), may hold values from -6 to 6
- dense_weight: bfloat16 [2048, 2048], P('shard'), may hold values from -2 to 2
- dense_bias: bfloat16 [2048], P('shard'), may hold values from -4 to 4
- fc1_weight: bfloat16 [2048, 8192], P('shard'), may hold values from -0.125 to 0.125
- fc1_bias: bfloat16 [8192], P('shard'), may hold values from -4 to 4
- fc2_weight: bfloat16 [8192, 2048], P('shard'), may hold values from -0.0625 to 0.0625
- fc2_bias: bfloat16 [2048], P('shard'), may hold values from -4 to 4
Outputs:
- mixed: bfloat16 [8192, 2048], P(('rep', 'shard'))
- token_grad: bfloat16 [8192, 2048], P(('rep', 'shard'))
- grad_ln_gain: float32 [2048], P('shard')
- grad_ln_bias: float32 [2048], P('shard')
- grad_qkv_weight: float32 [2048, 6144], P('shard')
- grad_qkv_bias: float32 [6144], P('shard')
- grad_dense_weight: float32 [2048, 2048], P('shard')
- grad_dense_bias: float32 [2048], P('shard')
- grad_fc1_weight: float32 [2048, 8192], P('shard')
- grad_fc1_bias: float32 [8192], P('shard')
- grad_fc2_weight: float32 [8192, 2048], P('shard')
- grad_fc2_bias: float32 [2048], P('shard')
Inputs may be any that keep to these rules, and one draw needn't show every extreme that they name: `seq_lengths`: for replica group r and micro-batch m, entry j is the length of the sequence that starts at block j, or 0 where block j continues the sequence before it. Entry 0 is positive. A sequence that starts at block j runs to the block before the next positive entry (or to the last block), b blocks, and its length is over 128 * (b - 1) and at most 128 * b; b is at most 8; some sequence has 1024 tokens. `placement_order`: each device's row for a micro-batch is a permutation; a value b sends that row to the device of shard index b // 16 of the same replica group.
All inputs are finite; a program needn't handle non-finite values.
Results may differ from a plain program's by a relative error of at most 0.013.
Values may be sent and summed in bfloat16 or wider, within the bound.
A program may use at most 704 MiB of HBM per device.

v0:
```python
import math

import jax
import jax.numpy as jnp
from jax import lax
from jax.sharding import PartitionSpec as P

HEADS = 32
HDIM = 64
ROT = 32
BLOCK = 128
MICRO = 2
MAXBLK = 8


def shifted(block, axis, distance):
    devices = range(lax.axis_size(axis))
    route = [(i - distance, i) for i in devices if i - distance in devices]
    return lax.ppermute(block, axis, route)


def contract_last(left, right):
    return lax.dot_general(
        left, right, (((1,), (1,)), ((), ())), preferred_element_type=jnp.float32
    )


def contract_first(left, right):
    return lax.dot_general(
        left, right, (((0,), (0,)), ((), ())), preferred_element_type=jnp.float32
    )


def normalize(inputs, gain_vec, bias_vec):
    average = jnp.mean(inputs, axis=-1, keepdims=True)
    centered = inputs - average
    variance = jnp.mean(centered * centered, axis=-1, keepdims=True)
    return centered * lax.rsqrt(variance + 1e-05) * gain_vec + bias_vec


def rotary_tables(position):
    half_dim = ROT // 2
    freqs = jnp.exp(-math.log(10000.0) * jnp.arange(half_dim, dtype=jnp.float32) * 2.0 / ROT)
    angles = position.astype(jnp.float32)[:, None] * freqs[None, :]
    angles = jnp.concatenate([angles, angles], axis=1)
    return (jnp.cos(angles)[:, None, :], jnp.sin(angles)[:, None, :])


def rotate(heads, cosine_table, sine_table):
    half_dim = ROT // 2
    turned_part = heads[..., :ROT]
    swapped = jnp.concatenate([-turned_part[..., half_dim:], turned_part[..., :half_dim]], axis=-1)
    return jnp.concatenate(
        [turned_part * cosine_table + swapped * sine_table, heads[..., ROT:]], axis=-1
    )


def gelu_tanh(values):
    return jax.nn.gelu(values, approximate=True)


def block_meta(lengths_row, first_row, span_rows):
    block_count = lengths_row.shape[0]
    blocks = jnp.arange(block_count, dtype=jnp.int32)
    begins = jnp.max(
        jnp.where(
            (lengths_row[None, :] > 0) & (blocks[None, :] <= blocks[:, None]), blocks[None, :], 0
        ),
        axis=1,
    )
    begin_length = jnp.sum(
        jnp.where(begins[:, None] == blocks[None, :], lengths_row[None, :], 0), axis=1
    )
    global_rows = first_row + jnp.arange(span_rows, dtype=jnp.int32)
    picks = (global_rows // BLOCK)[:, None] == blocks[None, :]
    segment = jnp.sum(jnp.where(picks, begins[None, :], 0), axis=1)
    limit = jnp.sum(jnp.where(picks, begin_length[None, :], 0), axis=1)
    position = global_rows - segment * BLOCK
    usable = (global_rows >= 0) & (position < limit)
    return (segment, position, usable)


def reduce_grads(hn_rows, dqkv_rows, dup_rows, ob_rows, gact_rows, gy_rows, vectors):
    wide = lax.psum_scatter(
        jnp.concatenate(
            [
                contract_first(hn_rows, dqkv_rows),
                contract_first(hn_rows, dup_rows),
                contract_first(ob_rows, gy_rows),
            ],
            axis=1,
        ).astype(jnp.bfloat16),
        "shard",
        scatter_dimension=0,
        tiled=True,
    ).astype(jnp.float32)
    deep = lax.psum_scatter(
        contract_first(gact_rows, gy_rows).astype(jnp.bfloat16),
        "shard",
        scatter_dimension=0,
        tiled=True,
    ).astype(jnp.float32)
    scattered = (
        lax.psum_scatter(
            vectors[0].astype(jnp.bfloat16), "shard", scatter_dimension=0, tiled=True
        ).astype(jnp.float32),
        lax.psum_scatter(
            vectors[1].astype(jnp.bfloat16), "shard", scatter_dimension=0, tiled=True
        ).astype(jnp.float32),
        lax.psum_scatter(
            vectors[2].astype(jnp.bfloat16), "shard", scatter_dimension=0, tiled=True
        ).astype(jnp.float32),
        lax.psum_scatter(
            vectors[3].astype(jnp.bfloat16), "shard", scatter_dimension=0, tiled=True
        ).astype(jnp.float32),
        lax.psum_scatter(
            vectors[4].astype(jnp.bfloat16), "shard", scatter_dimension=0, tiled=True
        ).astype(jnp.float32),
    )
    return lax.psum(
        (wide, deep, scattered[0], scattered[1], scattered[2], scattered[3], scattered[4]), "rep"
    )


def body(
    tokens,
    cotangent,
    placement_order,
    seq_lengths,
    ln_gain,
    ln_bias,
    qkv_weight,
    qkv_bias,
    dense_weight,
    dense_bias,
    fc1_weight,
    fc1_bias,
    fc2_weight,
    fc2_bias,
):
    group_size = lax.axis_size("shard")
    shard_pos = lax.axis_index("shard")
    model_width = tokens.shape[1]
    ff_width = fc1_weight.shape[1]
    row_count = tokens.shape[0] // MICRO
    cap_rows = row_count // group_size
    blk_dev = row_count // BLOCK
    reach = (MAXBLK - 1 + blk_dev - 1) // blk_dev
    span_rows = (reach + 1) * row_count
    scale = 1.0 / math.sqrt(HDIM)
    orders = placement_order[0, 0]
    micro_ids = jnp.arange(MICRO, dtype=jnp.int32)[:, None]
    spots = jnp.broadcast_to(jnp.arange(row_count, dtype=jnp.int32)[None, :], orders.shape)
    inverse = jnp.zeros_like(orders).at[micro_ids, orders].set(spots)

    def to_buffer(array):
        return jnp.take_along_axis(
            array.reshape(MICRO, row_count, model_width), inverse[:, :, None], axis=1
        ).reshape(MICRO, group_size, cap_rows, model_width)

    arrived = (
        lax.all_to_all(to_buffer(tokens), "shard", split_axis=1, concat_axis=1, tiled=True),
        lax.all_to_all(to_buffer(cotangent), "shard", split_axis=1, concat_axis=1, tiled=True),
    )
    att_x = arrived[0].reshape(MICRO, row_count, model_width)
    att_g = arrived[1].reshape(MICRO, row_count, model_width)
    shards = (
        ln_gain,
        ln_bias,
        qkv_weight,
        qkv_bias,
        dense_weight,
        dense_bias,
        fc1_weight,
        fc1_bias,
        fc2_weight,
        fc2_bias,
    )
    gathered_once = (
        lax.all_gather(shards[0], "shard", axis=0, tiled=True),
        lax.all_gather(shards[1], "shard", axis=0, tiled=True),
        lax.all_gather(shards[2], "shard", axis=0, tiled=True),
        lax.all_gather(shards[3], "shard", axis=0, tiled=True),
        lax.all_gather(shards[4], "shard", axis=0, tiled=True),
        lax.all_gather(shards[5], "shard", axis=0, tiled=True),
        lax.all_gather(shards[6], "shard", axis=0, tiled=True),
        lax.all_gather(shards[7], "shard", axis=0, tiled=True),
        lax.all_gather(shards[8], "shard", axis=0, tiled=True),
        lax.all_gather(shards[9], "shard", axis=0, tiled=True),
    )
    mixed_list = []
    grad_list = []
    stored = []
    totals = None
    for micro_idx in range(MICRO):
        gain_full, lnb_full, w_qkv, b_qkv, w_dense, b_dense, w_fc1, b_fc1, w_fc2, b_fc2 = (
            gathered_once
        )
        segment, position, usable = block_meta(
            seq_lengths[0, micro_idx], (shard_pos - reach) * row_count, span_rows
        )
        seg_query = segment[reach * row_count :]
        pos_query = position[reach * row_count :]
        valid_query = usable[reach * row_count :]
        inputs = att_x[micro_idx].astype(jnp.float32)
        normed, norm_pull = jax.vjp(
            normalize, inputs, gain_full.astype(jnp.float32), lnb_full.astype(jnp.float32)
        )
        hn_rows = normed.astype(jnp.bfloat16)
        qkv = jnp.dot(hn_rows, w_qkv, preferred_element_type=jnp.float32) + b_qkv.astype(
            jnp.float32
        )
        queries = qkv[:, :model_width].reshape(row_count, HEADS, HDIM)
        keys_raw = qkv[:, model_width : 2 * model_width].reshape(row_count, HEADS, HDIM)
        value_rows = qkv[:, 2 * model_width :].astype(jnp.bfloat16)
        cosine_table, sine_table = rotary_tables(pos_query)
        turned, turn_pull = jax.vjp(
            lambda first, second: (
                rotate(first, cosine_table, sine_table),
                rotate(second, cosine_table, sine_table),
            ),
            queries,
            keys_raw,
        )
        q_low = turned[0].astype(jnp.bfloat16)
        key_rows = turned[1].astype(jnp.bfloat16).reshape(row_count, model_width)
        older = []
        for shift_by in range(1, reach + 1):
            older.append(shifted((key_rows, value_rows), "shard", shift_by))
        key_win = jnp.concatenate(
            [received[0] for received in reversed(older)] + [key_rows], axis=0
        ).reshape(span_rows, HEADS, HDIM)
        val_win = jnp.concatenate(
            [received[1] for received in reversed(older)] + [value_rows], axis=0
        ).reshape(span_rows, HEADS, HDIM)
        allowed = (
            (seg_query[:, None] == segment[None, :])
            & (position[None, :] <= pos_query[:, None])
            & usable[None, :]
        )
        scores = (
            jnp.einsum("qhd,khd->hqk", q_low, key_win, preferred_element_type=jnp.float32) * scale
        )
        masked = jnp.where(allowed[None], scores, -1e30)
        top_score = jnp.max(masked, axis=-1, keepdims=True)
        expo = jnp.exp(masked - top_score)
        denom = jnp.sum(expo, axis=-1, keepdims=True)
        log_total = top_score + jnp.log(denom)
        probs = expo / denom
        attn_rows = jnp.einsum(
            "hqk,khd->qhd", probs.astype(jnp.bfloat16), val_win, preferred_element_type=jnp.float32
        )
        ob_rows = attn_rows.reshape(row_count, model_width).astype(jnp.bfloat16)
        attn_proj = jnp.dot(ob_rows, w_dense, preferred_element_type=jnp.float32) + b_dense.astype(
            jnp.float32
        )
        upper = jnp.dot(hn_rows, w_fc1, preferred_element_type=jnp.float32) + b_fc1.astype(
            jnp.float32
        )
        activated, gelu_pull = jax.vjp(gelu_tanh, upper)
        gact_rows = activated.astype(jnp.bfloat16)
        mlp_out = jnp.dot(gact_rows, w_fc2, preferred_element_type=jnp.float32) + b_fc2.astype(
            jnp.float32
        )
        mixed_rows = inputs + jnp.where(valid_query[:, None], attn_proj + mlp_out, 0.0)
        mixed_list.append(mixed_rows.astype(jnp.bfloat16))
        gy_rows = jnp.where(valid_query[:, None], att_g[micro_idx], jnp.zeros((), jnp.bfloat16))
        d_act = contract_last(gy_rows, w_fc2)
        dup_rows = gelu_pull(d_act)[0].astype(jnp.bfloat16)
        d_out = contract_last(gy_rows, w_dense).astype(jnp.bfloat16).reshape(row_count, HEADS, HDIM)
        again = (
            jnp.einsum("qhd,khd->hqk", q_low, key_win, preferred_element_type=jnp.float32) * scale
        )
        probs_again = jnp.where(allowed[None], jnp.exp(again - log_total), 0.0)
        d_probs = jnp.einsum("qhd,khd->hqk", d_out, val_win, preferred_element_type=jnp.float32)
        row_delta = jnp.sum(probs_again * d_probs, axis=-1, keepdims=True)
        d_scores = (probs_again * (d_probs - row_delta)).astype(jnp.bfloat16)
        d_query = (
            jnp.einsum("hqk,khd->qhd", d_scores, key_win, preferred_element_type=jnp.float32)
            * scale
        )
        d_keywin = (
            jnp.einsum("hqk,qhd->khd", d_scores, q_low, preferred_element_type=jnp.float32) * scale
        ).reshape(span_rows, model_width)
        d_valwin = jnp.einsum(
            "hqk,qhd->khd",
            probs_again.astype(jnp.bfloat16),
            d_out,
            preferred_element_type=jnp.float32,
        ).reshape(span_rows, model_width)
        key_total = d_keywin[reach * row_count :]
        value_total = d_valwin[reach * row_count :]
        for shift_by in range(1, reach + 1):
            lower_row = (reach - shift_by) * row_count
            returned = (
                shifted(
                    d_keywin[lower_row : lower_row + row_count].astype(jnp.bfloat16),
                    "shard",
                    -shift_by,
                ).astype(jnp.float32),
                shifted(
                    d_valwin[lower_row : lower_row + row_count].astype(jnp.bfloat16),
                    "shard",
                    -shift_by,
                ).astype(jnp.float32),
            )
            key_total = key_total + returned[0]
            value_total = value_total + returned[1]
        unturned = turn_pull((d_query, key_total.reshape(row_count, HEADS, HDIM)))
        dqkv_rows = jnp.concatenate(
            [
                unturned[0].reshape(row_count, model_width),
                unturned[1].reshape(row_count, model_width),
                value_total,
            ],
            axis=1,
        ).astype(jnp.bfloat16)
        d_normed = contract_last(dqkv_rows, w_qkv) + contract_last(dup_rows, w_fc1)
        d_inputs, d_gain, d_lnbias = norm_pull(d_normed)
        grad_list.append((att_g[micro_idx].astype(jnp.float32) + d_inputs).astype(jnp.bfloat16))
        vectors = (
            jnp.sum(dqkv_rows.astype(jnp.float32), axis=0),
            jnp.sum(dup_rows.astype(jnp.float32), axis=0),
            jnp.sum(gy_rows.astype(jnp.float32), axis=0),
            d_gain,
            d_lnbias,
        )
        stored.append((hn_rows, dqkv_rows, dup_rows, ob_rows, gact_rows, gy_rows, vectors))
    joined = [jnp.concatenate([entry[slot] for entry in stored], axis=0) for slot in range(6)]
    vector_sums = tuple(
        (jnp.sum(jnp.stack([entry[6][slot] for entry in stored]), axis=0) for slot in range(5))
    )
    totals = reduce_grads(
        joined[0], joined[1], joined[2], joined[3], joined[4], joined[5], vector_sums
    )
    mixed_back = jnp.stack(mixed_list).reshape(MICRO, group_size, cap_rows, model_width)
    grads_back = jnp.stack(grad_list).reshape(MICRO, group_size, cap_rows, model_width)
    homeward = (
        lax.all_to_all(mixed_back, "shard", split_axis=1, concat_axis=1, tiled=True),
        lax.all_to_all(grads_back, "shard", split_axis=1, concat_axis=1, tiled=True),
    )

    def from_buffer(array):
        return jnp.take_along_axis(
            array.reshape(MICRO, row_count, model_width), orders[:, :, None], axis=1
        ).reshape(MICRO * row_count, model_width)

    wide, deep, bias_qkv, bias_fc1, bias_out, gain_grad, lnbias_grad = totals
    qkv_cols = 3 * model_width
    return (
        from_buffer(homeward[0]),
        from_buffer(homeward[1]),
        gain_grad,
        lnbias_grad,
        wide[:, :qkv_cols],
        bias_qkv,
        wide[:, qkv_cols + ff_width :],
        bias_out,
        wide[:, qkv_cols : qkv_cols + ff_width],
        bias_fc1,
        deep,
        bias_out,
    )


def solution(mesh):
    placed = (
        P(("rep", "shard"), None),
        P(("rep", "shard"), None),
        P("rep", "shard", None, None),
        P("rep", None, None),
        P("shard"),
        P("shard"),
        P("shard", None),
        P("shard"),
        P("shard", None),
        P("shard"),
        P("shard", None),
        P("shard"),
        P("shard", None),
        P("shard"),
    )
    return jax.shard_map(
        body,
        mesh=mesh,
        in_specs=placed,
        out_specs=(
            P(("rep", "shard"), None),
            P(("rep", "shard"), None),
            P("shard"),
            P("shard"),
            P("shard", None),
            P("shard"),
            P("shard", None),
            P("shard"),
            P("shard", None),
            P("shard"),
            P("shard", None),
            P("shard"),
        ),
        check_vma=False,
    )
```

profile of v0, /device:TPU:0, one launch (start us, length us, event | category | flops | bytes accessed | tf_op | source)
XLA Modules:
  0.0 2567.8 jit_solution(3848046647579262749)
XLA Ops:
  10.6 11.4 scatter_fusion
  39.3 24.7 all-gather.1
  64.0 9.3 all-gather
  73.4 7.7 all_gather.37
  81.1 9.2 all-gather.2
  98.0 25.0 all-to-all-done.2
  140.5 74.5 %all-gather.10.cloned.1.call-done = bf16[2048,6144]{1,0:T(8,128)(2,1)} async-done(((bf16[256,6144]{1,0:T(8,128)(2,1)}), bf16[2048,6144]{1,0:T(8,128)(2,1)}) %all-gather.10.cloned.1.call-update) | async-done | bytes 25165840 | tf_op jit(solution)/shard_map/all_gather | solution.py:182
  215.1 10.0 convolution_add_fusion.3
  230.2 147.6 %all-gather.16.cloned.1.call-done = bf16[8192,2048]{1,0:T(8,128)(2,1)} async-done(((bf16[1024,2048]{1,0:T(8,128)(2,1)}), bf16[8192,2048]{1,0:T(8,128)(2,1)}) %all-gather.16.cloned.1.call-update) | async-done | bytes 33554448 | tf_op jit(solution)/shard_map/all_gather | solution.py:188
  377.8 19.8 fusion.171
  397.6 17.4 fusion.172
  415.0 125.3 %all-gather.14.cloned.1.call-done = bf16[2048,8192]{1,0:T(8,128)(2,1)} async-done(((bf16[256,8192]{1,0:T(8,128)(2,1)}), bf16[2048,8192]{1,0:T(8,128)(2,1)}) %all-gather.14.cloned.1.call-update) | async-done | bytes 33554448 | tf_op jit(solution)/shard_map/all_gather | solution.py:186
  540.4 18.5 convert_reduce_fusion.1
  558.9 18.6 convert_reduce_fusion
  577.5 16.2 convolution_convert_fusion
  609.5 14.5 convolution_add_fusion.2
  668.0 65.2 %collective-permute-done = bf16[128,2048]{1,0:T(8,128)(2,1)S(1)} collective-permute-done((bf16[128,2048]{1,0:T(8,128)(2,1)S(1)}, bf16[128,2048]{1,0:T(8,128)(2,1)S(1)}, u32[]{:S(2)}, u32[]{:S(2)}) %collective-permute-start) | collective-permute-done | bytes 524320 | tf_op jit(solution)/shard_map/ppermute | solution.py:19
  737.5 7.5 collective-permute-start.19
  745.8 17.2 collective-permute-done.3
  774.5 54.3 %collective-permute-done.14 = bf16[128,2048]{1,0:T(8,128)(2,1)S(1)} collective-permute-done((bf16[128,2048]{1,0:T(8,128)(2,1)S(1)}, bf16[128,2048]{1,0:T(8,128)(2,1)S(1)}, u32[]{:S(2)}, u32[]{:S(2)}) %collective-permute-start.14) | collective-permute-done | bytes 524320 | tf_op jit(solution)/shard_map/ppermute | solution.py:19
  840.2 16.6 collective-permute-done.17
  880.1 13.6 multiply_reduce_fusion.1
  893.8 13.5 multiply_convert_fusion.1
  915.4 10.4 fusion.167
  970.8 9.1 fusion.169
  981.1 13.7 multiply_reduce_fusion
  994.7 13.9 multiply_convert_fusion
  1020.9 7.8 fusion.63
  1035.6 9.8 fusion.65
  1077.2 20.7 collective-permute-done.48
  1104.8 16.7 collective-permute-done.44
  1124.9 23.6 collective-permute-done.41
  1167.8 25.6 collective-permute-done.55
  1197.3 13.6 collective-permute-done.52
  1212.3 15.1 convolution_convert_fusion.2
  1227.5 15.5 convolution_convert_fusion.1
  1242.9 44.7 %pad_maximum_fusion = bf16[2048,16384]{1,0:T(8,128)(2,1)} fusion(bf16[2048,2048]{1,0:T(8,128)(2,1)} %convolution_convert_fusion.3, bf16[2048,8192]{1,0:T(8,128)(2,1)} %convolution_convert_fusion.1, bf16[2048,6144]{1,0:T(8,128)(2,1)} %convolution_convert_fusion.2), kind=kLoop, calls=%fused_computation.5 | loop fusion | flops 201326592 | bytes 134217728 | tf_op jit(solution)/shard_map/concatenate | solution.py:85
  1291.1 17.5 all-gather.4
  1308.6 9.6 all-gather.3
  1335.9 22.8 fusion.97
  1358.7 18.8 fusion.96
  1377.5 19.0 fusion.61
  1396.5 15.1 fusion.62
  1418.3 17.7 convolution_add_fusion.4
  1436.1 19.8 multiply_reduce_fusion.3
  1462.2 45.2 %all-reduce.22 = (bf16[2048]{0:T(1024)(128)(2,1)S(1)}, bf16[2048]{0:T(1024)(128)(2,1)S(1)}, bf16[6144]{0:T(1024)(128)(2,1)S(1)}, bf16[2048]{0:T(1024)(128)(2,1)S(1)}, bf16[8192]{0:T(1024)(128)(2,1)S(1)}) all-reduce(bf16[2048]{0:T(1024)(128)(2,1)S(1)} %add_convert_fusion.12, ...), channel_id=2, replica_groups=mesh['rep'=4,'shard'=8] {'shard'}, use_global_device_ids=true, to_apply=%region_25.27.clone | all-reduce | flops 20480 | bytes 81920
  1519.4 186.6 %reduce-scatter.3.cloned.1.call-done = bf16[256,16384]{1,0:T(8,128)(2,1)} async-done(((bf16[2048,16384]{1,0:T(8,128)(2,1)}), bf16[256,16384]{1,0:T(8,128)(2,1)}) %reduce-scatter.3.cloned.1.call-update) | async-done | bytes 8388624 | tf_op jit(solution)/shard_map/reduce_scatter | solution.py:84
  1705.9 840.1 %all-reduce.24 = (f32[256]{0:T(256)}, f32[256]{0:T(256)}, f32[256,16384]{1,0:T(8,128)}, f32[768]{0:T(1024)}, f32[256]{0:T(256)S(1)}, /*index=5*/f32[1024]{0:T(1024)}, f32[1024,2048]{1,0:T(8,128)}) all-reduce(f32[256]{0:T(256)S(1)} %dynamic-slice_convert_fusion.4, ...), channel_id=1, replica_groups=mesh['rep'=4,'shard'=8] {'rep'}, use_global_device_ids=true, to_apply=%region_26.28 | all-reduce | flops 6294016 | bytes 37769216 | tf_op jit(solution)/shard_map/psum | solution.py:120
  (586 shorter events, 358.6 us)
Async XLA Ops:
  7.2 118.4 %all-gather.12.cloned.1.call-start = ((), (), s32[]{:S(2)}) async-start(), calls=%async_computation.7 | async-start | bytes 9437184 | tf_op jit(solution)/shard_map/all_gather | solution.py:184
  7.9 207.1 %all-gather.10.cloned.1.call-start = ((), (), s32[]{:S(2)}) async-start(), calls=%async_computation.6 | async-start | bytes 28311552 | tf_op jit(solution)/shard_map/all_gather | solution.py:182
  8.7 369.1 %all-gather.16.cloned.1.call-start = ((), (), s32[]{:S(2)}) async-start(), calls=%async_computation.9 | async-start | bytes 37748736 | tf_op jit(solution)/shard_map/all_gather | solution.py:188
  9.4 530.9 %all-gather.14.cloned.1.call-start = ((), (), s32[]{:S(2)}) async-start(), calls=%async_computation.8 | async-start | bytes 37748736 | tf_op jit(solution)/shard_map/all_gather | solution.py:186
  32.2 60.5 %all-to-all-start = ((bf16[2,8,16,2048]{3,2,0,1:T(8,128)(2,1)}), bf16[2,8,16,2048]{3,2,0,1:T(8,128)(2,1)S(1)}, u32[]{:S(2)}, u32[]{:S(2)}) async-start(bf16[2,8,16,2048]{3,2,0,1:T(8,128)(2,1)} %copy.92), calls=%async_computation | async-start | bytes 2097152 | tf_op jit(solution)/shard_map/all_to_all | solution.py:162
  96.2 1423.1 %reduce-scatter.5.cloned.1.call-start = ((), (), s32[]{:S(2)}) async-start(), calls=%async_computation.11 | async-start | bytes 37748736 | tf_op jit(solution)/shard_map/reduce_scatter | solution.py:97
  593.8 1112.2 %reduce-scatter.3.cloned.1.call-start = ((), (), s32[]{:S(2)}) async-start(), calls=%async_computation.10 | async-start | bytes 75497472 | tf_op jit(solution)/shard_map/reduce_scatter | solution.py:84
  595.0 55.4 %collective-permute-start.11 = (bf16[128,2048]{0,1:T(8,128)(2,1)}, bf16[128,2048]{0,1:T(8,128)(2,1)}, u32[]{:S(2)}, u32[]{:S(2)}) collective-permute-start(bf16[128,2048]{0,1:T(8,128)(2,1)} %bitcast.18), channel_id=1, source_target_pairs={{0,3},{1,4},{2,5},{3,6},{4,7},{8,11},{9,12},{10,13},{11,14},{12,15... | collective-permute-start | bytes 1572872 | tf_op jit(solution)/shard_map/ppermute | solution.py:19
  599.0 48.8 %collective-permute-start.10 = (bf16[128,2048]{0,1:T(8,128)(2,1)}, bf16[128,2048]{0,1:T(8,128)(2,1)}, u32[]{:S(2)}, u32[]{:S(2)}) collective-permute-start(bf16[128,2048]{0,1:T(8,128)(2,1)} %bitcast.18), channel_id=1, source_target_pairs={{0,4},{1,5},{2,6},{3,7},{8,12},{9,13},{10,14},{11,15},{16,20},{17,... | collective-permute-start | bytes 1572872 | tf_op jit(solution)/shard_map/ppermute | solution.py:19
  601.5 38.0 %collective-permute-start.9 = (bf16[128,2048]{0,1:T(8,128)(2,1)}, bf16[128,2048]{0,1:T(8,128)(2,1)}, u32[]{:S(2)}, u32[]{:S(2)}) collective-permute-start(bf16[128,2048]{0,1:T(8,128)(2,1)} %bitcast.18), channel_id=1, source_target_pairs={{0,5},{1,6},{2,7},{8,13},{9,14},{10,15},{16,21},{17,22},{18,23},{2... | collective-permute-start | bytes 1572872 | tf_op jit(solution)/shard_map/ppermute | solution.py:19
  603.6 33.2 %collective-permute-start.8 = (bf16[128,2048]{0,1:T(8,128)(2,1)}, bf16[128,2048]{0,1:T(8,128)(2,1)}, u32[]{:S(2)}, u32[]{:S(2)}) collective-permute-start(bf16[128,2048]{0,1:T(8,128)(2,1)} %bitcast.18), channel_id=1, source_target_pairs={{0,6},{1,7},{8,14},{9,15},{16,22},{17,23},{24,30},{25,31}} | collective-permute-start | bytes 1572872 | tf_op jit(solution)/shard_map/ppermute | solution.py:19
  639.4 128.6 %collective-permute-start.5 = (bf16[128,2048]{1,0:T(8,128)(2,1)S(1)}, bf16[128,2048]{1,0:T(8,128)(2,1)S(1)}, u32[]{:S(2)}, u32[]{:S(2)}) collective-permute-start(bf16[128,2048]{1,0:T(8,128)(2,1)S(1)} %slice.522), channel_id=1, source_target_pairs={{0,2},{1,3},{2,4},{3,5},{4,6},{5,7},{8,10},{9,11},{10,12},{11,13},... | collective-permute-start | bytes 1572872 | tf_op jit(solution)/shard_map/ppermute | solution.py:19
  647.8 118.1 %collective-permute-start.4 = (bf16[128,2048]{1,0:T(8,128)(2,1)S(1)}, bf16[128,2048]{1,0:T(8,128)(2,1)S(1)}, u32[]{:S(2)}, u32[]{:S(2)}) collective-permute-start(bf16[128,2048]{1,0:T(8,128)(2,1)S(1)} %slice.522), channel_id=1, source_target_pairs={{0,3},{1,4},{2,5},{3,6},{4,7},{8,11},{9,12},{10,13},{11,14},{12,15... | collective-permute-start | bytes 1572872 | tf_op jit(solution)/shard_map/ppermute | solution.py:19
  650.4 87.1 %collective-permute-start.2 = (bf16[128,2048]{1,0:T(8,128)(2,1)S(1)}, bf16[128,2048]{1,0:T(8,128)(2,1)S(1)}, u32[]{:S(2)}, u32[]{:S(2)}) collective-permute-start(bf16[128,2048]{1,0:T(8,128)(2,1)S(1)} %slice.522), channel_id=1, source_target_pairs={{0,5},{1,6},{2,7},{8,13},{9,14},{10,15},{16,21},{17,22},{18,23},{2... | collective-permute-start | bytes 1572872 | tf_op jit(solution)/shard_map/ppermute | solution.py:19
  655.3 80.0 %collective-permute-start.1 = (bf16[128,2048]{1,0:T(8,128)(2,1)S(1)}, bf16[128,2048]{1,0:T(8,128)(2,1)S(1)}, u32[]{:S(2)}, u32[]{:S(2)}) collective-permute-start(bf16[128,2048]{1,0:T(8,128)(2,1)S(1)} %slice.522), channel_id=1, source_target_pairs={{0,6},{1,7},{8,14},{9,15},{16,22},{17,23},{24,30},{25,31}} | collective-permute-start | bytes 1572872 | tf_op jit(solution)/shard_map/ppermute | solution.py:19
  656.9 76.3 %collective-permute-start = (bf16[128,2048]{1,0:T(8,128)(2,1)S(1)}, bf16[128,2048]{1,0:T(8,128)(2,1)S(1)}, u32[]{:S(2)}, u32[]{:S(2)}) collective-permute-start(bf16[128,2048]{1,0:T(8,128)(2,1)S(1)} %slice.522), channel_id=1, source_target_pairs={{0,7},{8,15},{16,23},{24,31}} | collective-permute-start | bytes 1572872 | tf_op jit(solution)/shard_map/ppermute | solution.py:19
  735.4 34.9 %collective-permute-start.6 = (bf16[128,2048]{1,0:T(8,128)(2,1)S(1)}, bf16[128,2048]{1,0:T(8,128)(2,1)S(1)}, u32[]{:S(2)}, u32[]{:S(2)}) collective-permute-start(bf16[128,2048]{1,0:T(8,128)(2,1)S(1)} %slice.522), channel_id=1, source_target_pairs={{0,1},{1,2},{2,3},{3,4},{4,5},{5,6},{6,7},{8,9},{9,10},{10,11},{11... | collective-permute-start | bytes 1572872 | tf_op jit(solution)/shard_map/ppermute | solution.py:19
  737.5 136.0 %collective-permute-start.19 = (bf16[128,2048]{1,0:T(8,128)(2,1)S(1)}, bf16[128,2048]{1,0:T(8,128)(2,1)}, u32[]{:S(2)}, u32[]{:S(2)}) collective-permute-start(bf16[128,2048]{1,0:T(8,128)(2,1)S(1)} %slice.521), channel_id=1, source_target_pairs={{0,2},{1,3},{2,4},{3,5},{4,6},{5,7},{8,10},{9,11},{10,12},{11,13},... | collective-permute-start | bytes 1572872 | tf_op jit(solution)/shard_map/ppermute | solution.py:19
  763.0 106.6 %collective-permute-start.18 = (bf16[128,2048]{1,0:T(8,128)(2,1)S(1)}, bf16[128,2048]{1,0:T(8,128)(2,1)}, u32[]{:S(2)}, u32[]{:S(2)}) collective-permute-start(bf16[128,2048]{1,0:T(8,128)(2,1)S(1)} %slice.521), channel_id=1, source_target_pairs={{0,3},{1,4},{2,5},{3,6},{4,7},{8,11},{9,12},{10,13},{11,14},{12,15... | collective-permute-start | bytes 1572872 | tf_op jit(solution)/shard_map/ppermute | solution.py:19
  765.9 68.0 %collective-permute-start.16 = (bf16[128,2048]{1,0:T(8,128)(2,1)S(1)}, bf16[128,2048]{1,0:T(8,128)(2,1)S(1)}, u32[]{:S(2)}, u32[]{:S(2)}) collective-permute-start(bf16[128,2048]{1,0:T(8,128)(2,1)S(1)} %slice.521), channel_id=1, source_target_pairs={{0,5},{1,6},{2,7},{8,13},{9,14},{10,15},{16,21},{17,22},{18,23},{2... | collective-permute-start | bytes 1572872 | tf_op jit(solution)/shard_map/ppermute | solution.py:19
  768.1 62.9 %collective-permute-start.15 = (bf16[128,2048]{1,0:T(8,128)(2,1)S(1)}, bf16[128,2048]{1,0:T(8,128)(2,1)S(1)}, u32[]{:S(2)}, u32[]{:S(2)}) collective-permute-start(bf16[128,2048]{1,0:T(8,128)(2,1)S(1)} %slice.521), channel_id=1, source_target_pairs={{0,6},{1,7},{8,14},{9,15},{16,22},{17,23},{24,30},{25,31}} | collective-permute-start | bytes 1572872 | tf_op jit(solution)/shard_map/ppermute | solution.py:19
  770.2 58.5 %collective-permute-start.14 = (bf16[128,2048]{1,0:T(8,128)(2,1)S(1)}, bf16[128,2048]{1,0:T(8,128)(2,1)S(1)}, u32[]{:S(2)}, u32[]{:S(2)}) collective-permute-start(bf16[128,2048]{1,0:T(8,128)(2,1)S(1)} %slice.521), channel_id=1, source_target_pairs={{0,7},{8,15},{16,23},{24,31}} | collective-permute-start | bytes 1572872 | tf_op jit(solution)/shard_map/ppermute | solution.py:19
  830.9 45.8 %collective-permute-start.20 = (bf16[128,2048]{1,0:T(8,128)(2,1)S(1)}, bf16[128,2048]{1,0:T(8,128)(2,1)}, u32[]{:S(2)}, u32[]{:S(2)}) collective-permute-start(bf16[128,2048]{1,0:T(8,128)(2,1)S(1)} %slice.521), channel_id=1, source_target_pairs={{0,1},{1,2},{2,3},{3,4},{4,5},{5,6},{6,7},{8,9},{9,10},{10,11},{11... | collective-permute-start | bytes 1572872 | tf_op jit(solution)/shard_map/ppermute | solution.py:19
  833.9 117.8 %collective-permute-start.25 = (bf16[128,2048]{0,1:T(8,128)(2,1)}, bf16[128,2048]{0,1:T(8,128)(2,1)S(1)}, u32[]{:S(2)}, u32[]{:S(2)}) collective-permute-start(bf16[128,2048]{0,1:T(8,128)(2,1)} %bitcast.37), channel_id=1, source_target_pairs={{0,3},{1,4},{2,5},{3,6},{4,7},{8,11},{9,12},{10,13},{11,14},{12,15... | collective-permute-start | bytes 1572872 | tf_op jit(solution)/shard_map/ppermute | solution.py:19
  856.8 92.7 %collective-permute-start.24 = (bf16[128,2048]{0,1:T(8,128)(2,1)}, bf16[128,2048]{0,1:T(8,128)(2,1)S(1)}, u32[]{:S(2)}, u32[]{:S(2)}) collective-permute-start(bf16[128,2048]{0,1:T(8,128)(2,1)} %bitcast.37), channel_id=1, source_target_pairs={{0,4},{1,5},{2,6},{3,7},{8,12},{9,13},{10,14},{11,15},{16,20},{17,... | collective-permute-start | bytes 1572872 | tf_op jit(solution)/shard_map/ppermute | solution.py:19
  869.5 76.9 %collective-permute-start.23 = (bf16[128,2048]{0,1:T(8,128)(2,1)}, bf16[128,2048]{0,1:T(8,128)(2,1)}, u32[]{:S(2)}, u32[]{:S(2)}) collective-permute-start(bf16[128,2048]{0,1:T(8,128)(2,1)} %bitcast.37), channel_id=1, source_target_pairs={{0,5},{1,6},{2,7},{8,13},{9,14},{10,15},{16,21},{17,22},{18,23},{2... | collective-permute-start | bytes 1572872 | tf_op jit(solution)/shard_map/ppermute | solution.py:19
  873.5 59.6 %collective-permute-start.22 = (bf16[128,2048]{0,1:T(8,128)(2,1)}, bf16[128,2048]{0,1:T(8,128)(2,1)S(1)}, u32[]{:S(2)}, u32[]{:S(2)}) collective-permute-start(bf16[128,2048]{0,1:T(8,128)(2,1)} %bitcast.37), channel_id=1, source_target_pairs={{0,6},{1,7},{8,14},{9,15},{16,22},{17,23},{24,30},{25,31}} | collective-permute-start | bytes 1572872 | tf_op jit(solution)/shard_map/ppermute | solution.py:19
  876.7 53.5 %collective-permute-start.21 = (bf16[128,2048]{0,1:T(8,128)(2,1)}, bf16[128,2048]{0,1:T(8,128)(2,1)S(1)}, u32[]{:S(2)}, u32[]{:S(2)}) collective-permute-start(bf16[128,2048]{0,1:T(8,128)(2,1)} %bitcast.37), channel_id=1, source_target_pairs={{0,7},{8,15},{16,23},{24,31}} | collective-permute-start | bytes 1572872 | tf_op jit(solution)/shard_map/ppermute | solution.py:19
  946.4 108.2 %collective-permute-start.34 = (bf16[128,2048]{0,1:T(8,128)(2,1)}, bf16[128,2048]{0,1:T(8,128)(2,1)}, u32[]{:S(2)}, u32[]{:S(2)}) collective-permute-start(bf16[128,2048]{0,1:T(8,128)(2,1)} %bitcast.71), channel_id=1, source_target_pairs={{7,0},{15,8},{23,16},{31,24}} | collective-permute-start | bytes 1572872 | tf_op jit(solution)/shard_map/ppermute | solution.py:19
  949.5 106.5 %collective-permute-start.28 = (bf16[128,2048]{0,1:T(8,128)(2,1)}, bf16[128,2048]{0,1:T(8,128)(2,1)}, u32[]{:S(2)}, u32[]{:S(2)}) collective-permute-start(bf16[128,2048]{0,1:T(8,128)(2,1)} %bitcast.65), channel_id=1, source_target_pairs={{1,0},{2,1},{3,2},{4,3},{5,4},{6,5},{7,6},{9,8},{10,9},{11,10},{12... | collective-permute-start | bytes 1572872 | tf_op jit(solution)/shard_map/ppermute | solution.py:19
  951.7 106.6 %collective-permute-start.33 = (bf16[128,2048]{0,1:T(8,128)(2,1)}, bf16[128,2048]{0,1:T(8,128)(2,1)}, u32[]{:S(2)}, u32[]{:S(2)}) collective-permute-start(bf16[128,2048]{0,1:T(8,128)(2,1)} %bitcast.70), channel_id=1, source_target_pairs={{6,0},{7,1},{14,8},{15,9},{22,16},{23,17},{30,24},{31,25}} | collective-permute-start | bytes 1572872 | tf_op jit(solution)/shard_map/ppermute | solution.py:19
  953.8 105.8 %collective-permute-start.32 = (bf16[128,2048]{0,1:T(8,128)(2,1)}, bf16[128,2048]{0,1:T(8,128)(2,1)}, u32[]{:S(2)}, u32[]{:S(2)}) collective-permute-start(bf16[128,2048]{0,1:T(8,128)(2,1)} %bitcast.69), channel_id=1, source_target_pairs={{5,0},{6,1},{7,2},{13,8},{14,9},{15,10},{21,16},{22,17},{23,18},{2... | collective-permute-start | bytes 1572872 | tf_op jit(solution)/shard_map/ppermute | solution.py:19
  957.0 104.0 %collective-permute-start.31 = (bf16[128,2048]{0,1:T(8,128)(2,1)}, bf16[128,2048]{0,1:T(8,128)(2,1)}, u32[]{:S(2)}, u32[]{:S(2)}) collective-permute-start(bf16[128,2048]{0,1:T(8,128)(2,1)} %bitcast.68), channel_id=1, source_target_pairs={{4,0},{5,1},{6,2},{7,3},{12,8},{13,9},{14,10},{15,11},{20,16},{21,... | collective-permute-start | bytes 1572872 | tf_op jit(solution)/shard_map/ppermute | solution.py:19
  1058.3 39.5 %collective-permute-start.48 = (bf16[128,2048]{0,1:T(8,128)(2,1)S(1)}, bf16[128,2048]{0,1:T(8,128)(2,1)S(1)}, u32[]{:S(2)}, u32[]{:S(2)}) collective-permute-start(bf16[128,2048]{0,1:T(8,128)(2,1)S(1)} %bitcast.361), channel_id=1, source_target_pairs={{7,0},{15,8},{23,16},{31,24}} | collective-permute-start | bytes 1572872 | tf_op jit(solution)/shard_map/ppermute | solution.py:19
  1059.6 39.5 %collective-permute-start.42 = (bf16[128,2048]{0,1:T(8,128)(2,1)S(1)}, bf16[128,2048]{0,1:T(8,128)(2,1)S(1)}, u32[]{:S(2)}, u32[]{:S(2)}) collective-permute-start(bf16[128,2048]{0,1:T(8,128)(2,1)S(1)} %bitcast.360), channel_id=1, source_target_pairs={{1,0},{2,1},{3,2},{4,3},{5,4},{6,5},{7,6},{9,8},{10,9},{11,10},{12... | collective-permute-start | bytes 1572872 | tf_op jit(solution)/shard_map/ppermute | solution.py:19
  1060.9 39.9 %collective-permute-start.47 = (bf16[128,2048]{0,1:T(8,128)(2,1)S(1)}, bf16[128,2048]{0,1:T(8,128)(2,1)S(1)}, u32[]{:S(2)}, u32[]{:S(2)}) collective-permute-start(bf16[128,2048]{0,1:T(8,128)(2,1)S(1)} %bitcast.359), channel_id=1, source_target_pairs={{6,0},{7,1},{14,8},{15,9},{22,16},{23,17},{30,24},{31,25}} | collective-permute-start | bytes 1572872 | tf_op jit(solution)/shard_map/ppermute | solution.py:19
  1068.2 34.0 %collective-permute-start.46 = (bf16[128,2048]{0,1:T(8,128)(2,1)S(1)}, bf16[128,2048]{0,1:T(8,128)(2,1)S(1)}, u32[]{:S(2)}, u32[]{:S(2)}) collective-permute-start(bf16[128,2048]{0,1:T(8,128)(2,1)S(1)} %bitcast.358), channel_id=1, source_target_pairs={{5,0},{6,1},{7,2},{13,8},{14,9},{15,10},{21,16},{22,17},{23,18},{2... | collective-permute-start | bytes 1572872 | tf_op jit(solution)/shard_map/ppermute | solution.py:19
  1100.8 47.6 %collective-permute-start.41 = (bf16[128,2048]{0,1:T(8,128)(2,1)S(1)}, bf16[128,2048]{0,1:T(8,128)(2,1)S(1)}, u32[]{:S(2)}, u32[]{:S(2)}) collective-permute-start(bf16[128,2048]{0,1:T(8,128)(2,1)S(1)} %bitcast.354), channel_id=1, source_target_pairs={{7,0},{15,8},{23,16},{31,24}} | collective-permute-start | bytes 1572872 | tf_op jit(solution)/shard_map/ppermute | solution.py:19
  1102.2 47.6 %collective-permute-start.35 = (bf16[128,2048]{0,1:T(8,128)(2,1)S(1)}, bf16[128,2048]{0,1:T(8,128)(2,1)S(1)}, u32[]{:S(2)}, u32[]{:S(2)}) collective-permute-start(bf16[128,2048]{0,1:T(8,128)(2,1)S(1)} %bitcast.353), channel_id=1, source_target_pairs={{1,0},{2,1},{3,2},{4,3},{5,4},{6,5},{7,6},{9,8},{10,9},{11,10},{12... | collective-permute-start | bytes 1572872 | tf_op jit(solution)/shard_map/ppermute | solution.py:19
  1103.5 48.9 %collective-permute-start.40 = (bf16[128,2048]{0,1:T(8,128)(2,1)S(1)}, bf16[128,2048]{0,1:T(8,128)(2,1)S(1)}, u32[]{:S(2)}, u32[]{:S(2)}) collective-permute-start(bf16[128,2048]{0,1:T(8,128)(2,1)S(1)} %bitcast.351), channel_id=1, source_target_pairs={{6,0},{7,1},{14,8},{15,9},{22,16},{23,17},{30,24},{31,25}} | collective-permute-start | bytes 1572872 | tf_op jit(solution)/shard_map/ppermute | solution.py:19
  1122.8 37.2 %collective-permute-start.38 = (bf16[128,2048]{0,1:T(8,128)(2,1)S(1)}, bf16[128,2048]{0,1:T(8,128)(2,1)S(1)}, u32[]{:S(2)}, u32[]{:S(2)}) collective-permute-start(bf16[128,2048]{0,1:T(8,128)(2,1)S(1)} %bitcast.348), channel_id=1, source_target_pairs={{4,0},{5,1},{6,2},{7,3},{12,8},{13,9},{14,10},{15,11},{20,16},{21,... | collective-permute-start | bytes 1572872 | tf_op jit(solution)/shard_map/ppermute | solution.py:19
  1152.3 41.1 %collective-permute-start.55 = (bf16[128,2048]{0,1:T(8,128)(2,1)S(1)}, bf16[128,2048]{0,1:T(8,128)(2,1)S(1)}, u32[]{:S(2)}, u32[]{:S(2)}) collective-permute-start(bf16[128,2048]{0,1:T(8,128)(2,1)S(1)} %bitcast.345), channel_id=1, source_target_pairs={{7,0},{15,8},{23,16},{31,24}} | collective-permute-start | bytes 1572872 | tf_op jit(solution)/shard_map/ppermute | solution.py:19
  1153.6 41.1 %collective-permute-start.49 = (bf16[128,2048]{0,1:T(8,128)(2,1)S(1)}, bf16[128,2048]{0,1:T(8,128)(2,1)S(1)}, u32[]{:S(2)}, u32[]{:S(2)}) collective-permute-start(bf16[128,2048]{0,1:T(8,128)(2,1)S(1)} %bitcast.344), channel_id=1, source_target_pairs={{1,0},{2,1},{3,2},{4,3},{5,4},{6,5},{7,6},{9,8},{10,9},{11,10},{12... | collective-permute-start | bytes 1572872 | tf_op jit(solution)/shard_map/ppermute | solution.py:19
  1160.0 37.3 %collective-permute-start.54 = (bf16[128,2048]{0,1:T(8,128)(2,1)S(1)}, bf16[128,2048]{0,1:T(8,128)(2,1)S(1)}, u32[]{:S(2)}, u32[]{:S(2)}) collective-permute-start(bf16[128,2048]{0,1:T(8,128)(2,1)S(1)} %bitcast.343), channel_id=1, source_target_pairs={{6,0},{7,1},{14,8},{15,9},{22,16},{23,17},{30,24},{31,25}} | collective-permute-start | bytes 1572872 | tf_op jit(solution)/shard_map/ppermute | solution.py:19
  1162.6 34.7 %collective-permute-start.53 = (bf16[128,2048]{0,1:T(8,128)(2,1)S(1)}, bf16[128,2048]{0,1:T(8,128)(2,1)S(1)}, u32[]{:S(2)}, u32[]{:S(2)}) collective-permute-start(bf16[128,2048]{0,1:T(8,128)(2,1)S(1)} %bitcast.342), channel_id=1, source_target_pairs={{5,0},{6,1},{7,2},{13,8},{14,9},{15,10},{21,16},{22,17},{23,18},{2... | collective-permute-start | bytes 1572872 | tf_op jit(solution)/shard_map/ppermute | solution.py:19
  1166.5 44.4 %collective-permute-start.52 = (bf16[128,2048]{0,1:T(8,128)(2,1)S(1)}, bf16[128,2048]{0,1:T(8,128)(2,1)S(1)}, u32[]{:S(2)}, u32[]{:S(2)}) collective-permute-start(bf16[128,2048]{0,1:T(8,128)(2,1)S(1)} %bitcast.341), channel_id=1, source_target_pairs={{4,0},{5,1},{6,2},{7,3},{12,8},{13,9},{14,10},{15,11},{20,16},{21,... | collective-permute-start | bytes 1572872 | tf_op jit(solution)/shard_map/ppermute | solution.py:19
  1414.0 44.5 %all-to-all-start.1 = ((bf16[2,8,16,2048]{3,2,0,1:T(8,128)(2,1)}), bf16[2,8,16,2048]{3,2,0,1:T(8,128)(2,1)}, u32[]{:S(2)}, u32[]{:S(2)}) async-start(bf16[2,8,16,2048]{3,2,0,1:T(8,128)(2,1)} %pad_maximum_fusion.3), calls=%async_computation.1 | async-start | bytes 2097152 | tf_op jit(solution)/shard_map/all_to_all | solution.py:339
  1458.5 54.9 %all-to-all-start.3 = ((bf16[2,8,16,2048]{3,2,0,1:T(8,128)(2,1)}), bf16[2,8,16,2048]{3,2,0,1:T(8,128)(2,1)S(1)}, u32[]{:S(2)}, u32[]{:S(2)}) async-start(bf16[2,8,16,2048]{3,2,0,1:T(8,128)(2,1)} %pad_maximum_fusion.4), calls=%async_computation.3 | async-start | bytes 2097152 | tf_op jit(solution)/shard_map/all_to_all | solution.py:340
  (150 other events, 6489.4 us)
Sparse Core Ops, SparseCore 0:
  9.9 66.3 all-gather.11
  78.2 136.8 all-gather.9
  217.0 160.7 all-gather.15
  379.5 160.7 all-gather.13
  593.9 311.8 reduce-scatter.4
  1287.9 417.9 reduce-scatter.2
where the time goes:
time: 2580 us; the launch traced here: 2570 us
  blocking collectives  963 us (37%)
  waiting for transfers between devices  836 us (32%)
  matrix products  385 us (15%)
  local copies, waits for them, and re-layouts  135 us (5%)
  starting transfers between devices  123 us (5%)
  other arithmetic  106 us (4%)
    psum x1, blocking collectives, reduce_grads(): lax.psum((wide, deep, scattered[0], scattered[1], scattered[2], scattered...  840 us
    ppermute x56, waiting for transfers between devices, shifted(): return lax.ppermute(block, axis, route)  275 us
    reduce_scatter x1, waiting for transfers between devices, reduce_grads(): lax.psum_scatter(jnp.concatenate([contract_first(hn_rows, dqkv_rows), con...  187 us
    all_gather x1, waiting for transfers between devices, body(): lax.all_gather(shards[8], 'shard', axis=0, tiled=True)  148 us
    dot_general x8, matrix products, contract_last(): lax.dot_general(left, right, (((1,), (1,)), ((), ())), preferred_element_...  129 us
    all_gather x1, waiting for transfers between devices, body(): lax.all_gather(shards[6], 'shard', axis=0, tiled=True)  125 us
    ppermute x56, starting transfers between devices, shifted(): return lax.ppermute(block, axis, route)  106 us
    all_gather x1, waiting for transfers between devices, body(): lax.all_gather(shards[2], 'shard', axis=0, tiled=True)  74.5 us
  transfers between devices with their start and end apart: 66, of which 22 were waited for; matrix products, arithmetic and copies ran while one was open for 21% of the time, Pallas kernels for 0%

commit v1 on v0

v1 whole, which is shorter than its diff:
```python
import functools
import math

import jax
import jax.numpy as jnp
from jax import lax
from jax.experimental import pallas as pl
from jax.experimental.pallas import tpu as pltpu
from jax.sharding import PartitionSpec as P

HEADS = 32
HDIM = 64
ROT = 32
BLOCK = 128
MICRO = 2
MAXBLK = 8
PAIR = 2 * HDIM
NEG = -1e30


def dot(left, right, dims, out=jnp.float32):
    return lax.dot_general(left, right, (dims, ((), ())), preferred_element_type=out)


def block_begins(lengths):
    blocks = jnp.arange(lengths.shape[1], dtype=jnp.int32)
    started = (lengths[:, None, :] > 0) & (blocks[None, None, :] <= blocks[None, :, None])
    begins = jnp.max(jnp.where(started, blocks[None, None, :], 0), axis=2)
    own = begins[:, :, None] == blocks[None, None, :]
    limits = jnp.sum(jnp.where(own, lengths[:, None, :], 0), axis=2)
    return begins, limits


def attention_kernel(begin_ref, q_ref, k_ref, v_ref, do_ref, cos_ref, low_ref, high_ref, kid_ref,
                     ob_ref, dq_ref, dk_ref, dv_ref, ks, vs, dks, dvs):
    micro = pl.program_id(0)
    blocks = q_ref.shape[1]
    lane = lax.broadcasted_iota(jnp.int32, (BLOCK, PAIR), 1)
    half = ROT // 2

    def rows(ref, j):
        return ref[:, j].reshape(BLOCK, PAIR)

    def table(ref, j):
        return ref[j * BLOCK:(j + 1) * BLOCK, :]

    def turn(x, j, back):
        up = pltpu.roll(x, PAIR - half, 1)
        down = pltpu.roll(x, half, 1)
        low, high = table(low_ref, j), table(high_ref, j)
        if back:
            return x * table(cos_ref, j) - up * low - down * high
        return x * table(cos_ref, j) + up * low + down * high

    for j in range(blocks):
        ks[j * BLOCK:(j + 1) * BLOCK, :] = turn(rows(k_ref, j), j, False).astype(jnp.bfloat16)
        vs[j * BLOCK:(j + 1) * BLOCK, :] = rows(v_ref, j).astype(jnp.bfloat16)
    dks[...] = jnp.zeros_like(dks)
    dvs[...] = jnp.zeros_like(dvs)
    causal = lax.broadcasted_iota(jnp.int32, (BLOCK, BLOCK), 1) <= lax.broadcasted_iota(
        jnp.int32, (BLOCK, BLOCK), 0
    )
    scale = 1.0 / math.sqrt(HDIM)
    zero = jnp.zeros((), jnp.bfloat16)
    for j in range(blocks):
        first = max(0, j - MAXBLK + 1)
        span = slice(first * BLOCK, (j + 1) * BLOCK)
        q_all = turn(rows(q_ref, j), j, False).astype(jnp.bfloat16)
        do_all = rows(do_ref, j).astype(jnp.bfloat16)
        keys, values = ks[span, :], vs[span, :]
        same = kid_ref[:, span] == begin_ref[micro, j]
        bias = jnp.where(same, 0.0, NEG)
        width = (j + 1 - first) * BLOCK
        outs, dqs = [], []
        for head in range(PAIR // HDIM):
            mine = (lane >= head * HDIM) & (lane < (head + 1) * HDIM)
            q = jnp.where(mine, q_all, zero)
            do = jnp.where(mine, do_all, zero)
            scores = dot(q, keys, ((1,), (1,))) * scale + bias
            tail = jnp.where(causal, scores[:, width - BLOCK:], NEG)
            if width > BLOCK:
                scores = jnp.concatenate([scores[:, :width - BLOCK], tail], axis=1)
            else:
                scores = tail
            top = jnp.max(scores, axis=1, keepdims=True)
            expo = jnp.exp(scores - top)
            probs = expo / jnp.sum(expo, axis=1, keepdims=True)
            low_probs = probs.astype(jnp.bfloat16)
            outs.append(dot(low_probs, values, ((1,), (0,))))
            dprobs = dot(do, values, ((1,), (1,)))
            weighted = probs * dprobs
            delta = jnp.sum(weighted, axis=1, keepdims=True)
            dscores = (weighted - probs * delta).astype(jnp.bfloat16)
            dqs.append(dot(dscores, keys, ((1,), (0,))))
            dks[span, :] += dot(dscores, q, ((0,), (0,)))
            dvs[span, :] += dot(low_probs, do, ((0,), (0,)))
        first_head = lane < HDIM
        shape = (q_ref.shape[0], q_ref.shape[2], PAIR)
        ob = jnp.where(first_head, outs[0], outs[1])
        ob_ref[:, j] = ob.astype(jnp.bfloat16).astype(jnp.float32).reshape(shape)
        dq = turn(jnp.where(first_head, dqs[0], dqs[1]) * scale, j, True)
        dq_ref[:, j] = dq.astype(jnp.bfloat16).astype(jnp.float32).reshape(shape)
    for j in range(blocks):
        here = slice(j * BLOCK, (j + 1) * BLOCK)
        shape = (q_ref.shape[0], q_ref.shape[2], PAIR)
        dk = turn(dks[here, :] * scale, j, True)
        dk_ref[:, j] = dk.astype(jnp.bfloat16).astype(jnp.float32).reshape(shape)
        dv_ref[:, j] = dvs[here, :].astype(jnp.bfloat16).astype(jnp.float32).reshape(shape)


def attention(begins, qkv, dout, cosine, low, high, kid):
    group, micros, blocks, cap, _ = qkv.shape
    width = dout.shape[-1]
    pairs = width // PAIR
    total = blocks * BLOCK

    def rows_spec(offset):
        return pl.BlockSpec(
            (group, None, blocks, cap, PAIR), lambda m, p, *_: (0, m, 0, 0, offset + p)
        )

    table_spec = pl.BlockSpec((None, total, PAIR), lambda m, p, *_: (m, 0, 0))
    out = jax.ShapeDtypeStruct(dout.shape, jnp.float32)
    work = micros * pairs * 2 * blocks * (min(blocks, MAXBLK) + 1) // 2 * BLOCK * BLOCK
    return pl.pallas_call(
        attention_kernel,
        grid_spec=pltpu.PrefetchScalarGridSpec(
            num_scalar_prefetch=1,
            grid=(micros, pairs),
            in_specs=[
                rows_spec(0), rows_spec(pairs), rows_spec(2 * pairs), rows_spec(0),
                table_spec, table_spec, table_spec,
                pl.BlockSpec((None, 1, total), lambda m, p, *_: (m, 0, 0)),
            ],
            out_specs=[rows_spec(0)] * 4,
            scratch_shapes=[
                pltpu.VMEM((total, PAIR), jnp.bfloat16),
                pltpu.VMEM((total, PAIR), jnp.bfloat16),
                pltpu.VMEM((total, PAIR), jnp.float32),
                pltpu.VMEM((total, PAIR), jnp.float32),
            ],
        ),
        out_shape=[out] * 4,
        compiler_params=pltpu.CompilerParams(vmem_limit_bytes=48 << 20),
        cost_estimate=pl.CostEstimate(
            flops=12 * work * PAIR, bytes_accessed=8 * dout.size * 4, transcendentals=work
        ),
    )(begins, qkv, qkv, qkv, dout, cosine, low, high, kid)


def body(
    tokens, cotangent, placement_order, seq_lengths, ln_gain, ln_bias, qkv_weight, qkv_bias,
    dense_weight, dense_bias, fc1_weight, fc1_bias, fc2_weight, fc2_bias,
):
    bf16, f32 = jnp.bfloat16, jnp.float32
    group = lax.axis_size("shard")
    reps = lax.axis_size("rep")
    me = lax.axis_index("shard")
    width = tokens.shape[1]
    rows = tokens.shape[0] // MICRO
    cap = rows // group
    mine = width // group
    ff_mine = fc1_weight.shape[1] // group
    blocks = seq_lengths.shape[2]
    all_rows = MICRO * rows * group

    pieces = (ln_gain, ln_bias, dense_bias, fc2_bias, qkv_bias, fc1_bias)
    packed = jnp.concatenate(pieces)
    spread = lax.all_gather(packed, "shard", axis=0).astype(f32)
    full, at = [], 0
    for piece in pieces:
        full.append(spread[:, at:at + piece.shape[0]].reshape(-1))
        at += piece.shape[0]
    gain, lnb, b_dense, b_fc2, b_qkv, b_fc1 = full
    b_qkv = lax.dynamic_slice_in_dim(b_qkv.reshape(3, width), me * mine, mine, 1).reshape(-1)
    b_fc1 = lax.dynamic_slice_in_dim(b_fc1, me * ff_mine, ff_mine, 0)

    fc1 = lax.all_to_all(
        fc1_weight.reshape(mine, group, ff_mine).transpose(1, 0, 2), "shard", 0, 0, tiled=True
    ).reshape(width, ff_mine)
    w_qkv = lax.all_to_all(
        qkv_weight.reshape(mine, 3, group, mine).transpose(2, 0, 1, 3), "shard", 0, 0, tiled=True
    ).reshape(width, 3 * mine)

    begins, limits = block_begins(seq_lengths[0])
    spot = jnp.arange(BLOCK, dtype=jnp.int32)
    index = jnp.arange(blocks, dtype=jnp.int32)
    position = (index[None, :, None] - begins[:, :, None]) * BLOCK + spot[None, None, :]
    valid = position < limits[:, :, None]
    key_id = jnp.where(valid, begins[:, :, None], -1).reshape(MICRO, 1, blocks * BLOCK)
    lane = jnp.arange(PAIR, dtype=jnp.int32) % HDIM
    half = ROT // 2
    freqs = jnp.exp(-math.log(10000.0) * jnp.arange(half, dtype=f32) * 2.0 / ROT)
    angles = position.reshape(MICRO, -1, 1).astype(f32) * freqs[lane % half]
    sines = jnp.sin(angles)
    cosine = jnp.where(lane < ROT, jnp.cos(angles), 1.0)
    low = jnp.where(lane < half, -sines, 0.0)
    high = jnp.where((lane >= half) & (lane < ROT), sines, 0.0)

    orders = placement_order[0, 0]
    select = (orders[:, None, :] == jnp.arange(rows, dtype=jnp.int32)[None, :, None]).astype(bf16)

    def arrange(array):
        return jnp.einsum(
            "mti,mid->mtd", select, array.reshape(MICRO, rows, width),
            preferred_element_type=f32,
        ).astype(bf16).reshape(MICRO * rows, width)

    x_home, g_home = arrange(tokens), arrange(cotangent)
    valid_home = lax.dynamic_index_in_dim(
        valid.reshape(MICRO, group, group, cap), me, 2, keepdims=False
    ).reshape(MICRO * rows, 1)
    gy_home = jnp.where(valid_home, g_home, jnp.zeros((), bf16))
    x32 = x_home.astype(f32)
    centered = x32 - jnp.mean(x32, axis=1, keepdims=True)
    rstd = lax.rsqrt(jnp.mean(centered * centered, axis=1, keepdims=True) + 1e-05)
    hn_home = (centered * rstd * gain + lnb).astype(bf16)
    gy = lax.all_gather(gy_home, "shard", axis=0, tiled=True)
    hn = lax.all_gather(hn_home, "shard", axis=0, tiled=True)

    upper = dot(hn, fc1, ((1,), (0,))) + b_fc1
    inner = math.sqrt(2.0 / math.pi) * (upper + 0.044715 * upper * upper * upper)
    curve = jnp.tanh(inner)
    act = (0.5 * upper * (1.0 + curve)).astype(bf16)
    slope = 0.5 * (1.0 + curve) + 0.5 * upper * (1.0 - curve * curve) * math.sqrt(
        2.0 / math.pi
    ) * (1.0 + 3 * 0.044715 * upper * upper)
    dup = (dot(gy, fc2_weight, ((1,), (1,))) * slope).astype(bf16)
    g_fc2 = dot(act, gy, ((0,), (0,)), f32).astype(bf16)
    g_fc1 = dot(hn, dup, ((0,), (0,)), f32).astype(bf16)

    def over_reps(part):
        return lax.psum_scatter(part, "rep", scatter_dimension=0, tiled=True)

    def from_reps(part):
        return lax.all_gather(part, "rep", axis=0, tiled=True)

    def by_rows(grad):
        cols = grad.shape[1]
        split = grad.reshape(group, reps, mine // reps, cols).transpose(1, 0, 2, 3)
        part = over_reps(split.reshape(reps * group, mine // reps, cols))
        part = lax.all_to_all(part, "shard", 0, 0, tiled=True)
        whole = from_reps(part)
        return whole.reshape(reps, group, mine // reps, cols)

    grad_fc2 = from_reps(over_reps(g_fc2)).astype(f32)
    grad_fc1 = by_rows(g_fc1).transpose(0, 2, 1, 3).reshape(mine, -1).astype(f32)

    qkv = dot(hn, w_qkv, ((1,), (0,))) + b_qkv
    dout = dot(gy, dense_weight, ((1,), (1,)))
    shape = (group, MICRO, blocks, cap)
    ob, dq, dk, dv = attention(
        begins, qkv.reshape(*shape, 3 * mine), dout.reshape(*shape, mine), cosine, low, high,
        key_id,
    )
    ob = ob.reshape(all_rows, mine).astype(bf16)
    dqkv = jnp.concatenate(
        [part.reshape(all_rows, mine).astype(bf16) for part in (dq, dk, dv)], axis=1
    )
    g_qkv = dot(hn, dqkv, ((0,), (0,)), f32).astype(bf16)
    g_dense = dot(ob, gy, ((0,), (0,)), f32).astype(bf16)
    grad_dense = from_reps(over_reps(g_dense)).astype(f32)
    grad_qkv = by_rows(g_qkv).reshape(reps, group, mine // reps, 3, mine)
    grad_qkv = grad_qkv.transpose(0, 2, 3, 1, 4).reshape(mine, 3 * width).astype(f32)

    def home(part):
        got = lax.all_to_all(part.reshape(group, MICRO * rows, width), "shard", 0, 0, tiled=True)
        return jnp.sum(got.astype(f32), axis=0)

    out_part = (
        dot(act, fc2_weight, ((1,), (0,))) + dot(ob, dense_weight, ((1,), (0,)))
    ).astype(bf16)
    dh_part = (dot(dqkv, w_qkv, ((1,), (1,))) + dot(dup, fc1, ((1,), (1,)))).astype(bf16)
    branch = home(out_part) + (b_dense + b_fc2)
    mixed = (x32 + jnp.where(valid_home, branch, 0.0)).astype(bf16)
    dh = home(dh_part)
    xhat = centered * rstd
    scaled = dh * gain
    dx = (
        scaled
        - jnp.mean(scaled, axis=1, keepdims=True)
        - xhat * jnp.mean(scaled * xhat, axis=1, keepdims=True)
    ) * rstd
    token_grad = (g_home.astype(f32) + dx).astype(bf16)

    def back(array):
        return jnp.einsum(
            "mti,mtd->mid", select, array.reshape(MICRO, rows, width),
            preferred_element_type=f32,
        ).astype(bf16).reshape(MICRO * rows, width)

    def placed(part, count, offset):
        return lax.dynamic_update_slice_in_dim(
            jnp.zeros((count,) + part.shape[1:], f32), part, offset, 0
        )

    v_qkv = jnp.sum(dqkv.astype(f32), axis=0).reshape(3, mine).T
    v_qkv = placed(v_qkv, width, me * mine).T.reshape(-1)
    v_fc1 = placed(jnp.sum(dup.astype(f32), axis=0), group * ff_mine, me * ff_mine)
    v_out = jnp.sum(gy_home.astype(f32), axis=0)
    v_gain = jnp.sum(dh * xhat, axis=0)
    v_lnb = jnp.sum(dh, axis=0)
    sums = lax.psum(jnp.concatenate([v_qkv, v_fc1, v_out, v_gain, v_lnb]), ("rep", "shard"))
    outs, at = [], 0
    for count in (3 * width, group * ff_mine, width, width, width):
        share = count // group
        outs.append(lax.dynamic_slice_in_dim(sums, at + me * share, share, 0))
        at += count
    bias_qkv, bias_fc1, bias_out, gain_grad, lnb_grad = outs
    return (
        back(mixed), back(token_grad), gain_grad, lnb_grad, grad_qkv, bias_qkv, grad_dense,
        bias_out, grad_fc1, bias_fc1, grad_fc2, bias_out,
    )


def solution(mesh):
    rows = P(("rep", "shard"), None)
    vector, matrix = P("shard"), P("shard", None)
    layer = (vector, vector, matrix, vector, matrix, vector, matrix, vector, matrix, vector)
    return jax.shard_map(
        body,
        mesh=mesh,
        in_specs=(rows, rows, P("rep", "shard", None, None), P("rep", None, None)) + layer,
        out_specs=(rows, rows) + layer,
        check_vma=False,
    )
```

time: 2580 us -> 940 us (0.36)
  blocking collectives: 963 us -> 10.7 us
  waiting for transfers between devices: 836 us -> 518 us
  matrix products: 385 us -> 156 us
  starting transfers between devices: 123 us -> 28.3 us
  Pallas kernels: 0 us -> 54.9 us
  other arithmetic: 106 us -> 55.3 us
  local copies, waits for them, and re-layouts: 135 us -> 95.9 us
    psum x1 -> x0, blocking collectives: 840 us -> none  [reduce_grads(): lax.psum((wide, deep, scattered[0], scattered[1], scattered[2], scattered...]
    ppermute x56 -> x0, waiting for transfers between devices: 275 us -> none  [shifted(): return lax.ppermute(block, axis, route)]
    all_to_all x4 -> x6, waiting for transfers between devices: 25 us -> 259 us  [the longest x2 181 us: home(): lax.all_to_all(part.reshape(group, MICRO * rows, width), 'shard', 0, 0, t...]
    dot_general x32 -> x16, matrix products: 385 us -> 156 us  [the longest x12 148 us: dot(): lax.dot_general(left, right, (dims, ((), ())), preferred_element_type=out)]
    reduce_scatter x2 -> x4, waiting for transfers between devices: 187 us -> 0.06 us  [over_reps(): return lax.psum_scatter(part, 'rep', scatter_dimension=0, tiled=True)]
    all_gather x4 -> x6, waiting for transfers between devices: 348 us -> 235 us  [the longest x4 191 us: from_reps(): return lax.all_gather(part, 'rep', axis=0, tiled=True)]
    ppermute x56 -> x0, starting transfers between devices: 106 us -> none  [shifted(): return lax.ppermute(block, axis, route)]
    all_gather x6 -> x1, blocking collectives: 77.9 us -> 10.7 us  [body(): spread = lax.all_gather(packed, 'shard', axis=0).astype(f32)]
  transfers between devices with their start and end apart: 66 -> 17, of which waited for: 22 -> 11; matrix products, arithmetic and copies ran while one was open for 21% -> 28% of each run, Pallas kernels for 0% -> 0%
where the time goes in v1:
time: 940 us; the launch traced here: 933 us
  waiting for transfers between devices  518 us (55%)
  matrix products  156 us (17%)
  local copies, waits for them, and re-layouts  95.9 us (10%)
  other arithmetic  55.3 us (6%)
  Pallas kernels  54.9 us (6%)
  starting transfers between devices  28.3 us (3%)
  between operations  14.8 us (2%)
  blocking collectives  10.7 us (1%)
    all_gather x4, waiting for transfers between devices, from_reps(): return lax.all_gather(part, 'rep', axis=0, tiled=True)  191 us
    all_to_all x2, waiting for transfers between devices, home(): lax.all_to_all(part.reshape(group, MICRO * rows, width), 'shard', 0, 0, t...  181 us
    dot_general x12, matrix products, dot(): lax.dot_general(left, right, (dims, ((), ())), preferred_element_type=out)  148 us
    pallas_call x1, Pallas kernels, attention(): pl.pallas_call(attention_kernel, grid_spec=pltpu.PrefetchScalarGridSpec(n...  54.9 us
    all_gather x1, waiting for transfers between devices, body(): hn = lax.all_gather(hn_home, 'shard', axis=0, tiled=True)  44.4 us
    all_to_all x1, waiting for transfers between devices, body(): lax.all_to_all(qkv_weight.reshape(mine, 3, group, mine).transpose(2, 0, 1...  39.3 us
    unnamed x76, local copies, waits for them, and re-layouts  39 us
    all_to_all x1, waiting for transfers between devices, body(): lax.all_to_all(fc1_weight.reshape(mine, group, ff_mine).transpose(1, 0, 2...  32 us
  transfers between devices with their start and end apart: 17, of which 11 were waited for; matrix products, arithmetic and copies ran while one was open for 28% of the time, Pallas kernels for 0%

profile of v1, /device:TPU:0, one launch (start us, length us, event | category | flops | bytes accessed | tf_op | source)
XLA Modules:
  0.0 933.4 jit_solution(13279506254519524466)
XLA Ops:
  19.1 10.7 %all-gather.1 = bf16[8,1,2816]{2,1,0:T(2,128)(2,1)S(1)} all-gather(bf16[1,1,2816]{2,1,0:T(2,128)(2,1)S(1)} %reshape.519), channel_id=2, replica_groups=mesh['rep'=4,'shard'=8] {'shard'}, dimensions={0}, use_global_device_ids=true | all-gather | bytes 50688 | tf_op jit(solution)/shard_map/all_gather | solution.py:169
  35.3 4.6 copy.65
  39.9 3.9 copy.66
  43.8 4.5 all-to-all-start.1
  49.3 10.2 %bitcast_select_fusion.9 = f32[128]{0:T(128)S(1)} fusion(f32[]{:T(128)} %bitcast.34, f32[]{:T(128)} %bitcast.35, f32[]{:T(128)} %bitcast.36, f32[]{:T(128)} %bitcast.37, f32[]{:T(128)} %bitcast.38, f32[]{:T(128)} %bitcast.40, f32[]{:T(128)} %bitcast.39, f32[]{:T(128)} %bitcast.17, f32[]{:T(128)} %bitcast.19, f32[]{:T(128)} %bitcast.21, f32[]{:T(128)} %bitcast.23, ...), kind=kLoop, calls=%fused_computation.97 | loop fusion | flops 6400 | bytes 576 | tf_op jit(solution)/shard_map/gather | solution.py:194
  59.9 4.8 fusion.12
  64.7 39.3 %all-to-all-done.1 = bf16[8,256,3,256]{1,3,2,0:T(8,128)(2,1)} async-done(((bf16[8,256,3,256]{1,3,2,0:T(8,128)(2,1)}), bf16[8,256,3,256]{1,3,2,0:T(8,128)(2,1)}, u32[]{:S(2)}, u32[]{:S(2)}) %all-to-all-start.1) | async-done | bytes 3145760 | tf_op jit(solution)/shard_map/all_to_all | solution.py:181
  104.0 3.7 copy.67
  110.4 7.1 fusion.41
  117.5 44.4 %all-gather.9.cloned.1.call-done = bf16[2048,2048]{1,0:T(8,128)(2,1)} async-done(((bf16[256,2048]{1,0:T(8,128)(2,1)}), bf16[2048,2048]{1,0:T(8,128)(2,1)}) %all-gather.9.cloned.1.call-update) | async-done | bytes 8388624 | tf_op jit(solution)/shard_map/all_gather | solution.py:219
  161.9 11.8 %broadcast_add_fusion = f32[2048,768]{1,0:T(8,128)} fusion(f32[768]{0:T(1024)S(1)} %add.245, bf16[2048,2048]{1,0:T(8,128)(2,1)} %all-gather.9.cloned.1.call-done, bf16[2048,768]{0,1:T(8,128)(2,1)} %bitcast.209), kind=kOutput, calls=%fused_computation.22 | convolution fusion | flops 6444023808 | bytes 17828864 | tf_op jit(solution)/shard_map/dot_general | solution.py:22
  173.7 54.9 %shard_map.229 = (f32[8,2,8,16,256]{4,3,2,1,0:T(8,128)S(1)}, f32[8,2,8,16,256]{4,3,2,1,0:T(8,128)}, f32[8,2,8,16,256]{4,3,2,1,0:T(8,128)}, f32[8,2,8,16,256]{4,3,2,1,0:T(8,128)}) custom-call(s32[2,8]{1,0:T(2,128)S(1)} %select_reduce_fusion.1.begin_ref, f32[8,2,8,16,768]{4,3,2,1,0:T(8,128)} %bitcast.235, f32[8,2,8,16,768]{4,3,2,1,0:T(8,128)} %bitcast.236, ...), custom_call_target="tpu_custom_call" | custom-call | flops 7247757312 | bytes 16777216 | tf_op jit(solution)/shard_map/pallas_call | solution.py:125
  229.7 3.3 convolution_convert_fusion.7
  233.0 6.4 copy.63
  239.4 4.6 all-to-all-start
  249.3 9.8 %convolution_convert_fusion.2 = bf16[2048,768]{1,0:T(8,128)(2,1)S(1)} fusion(bf16[2048,2048]{1,0:T(8,128)(2,1)} %all-gather.9.cloned.1.call-done, bf16[2048,256]{1,0:T(8,128)(2,1)S(1)} %bitcast.203, bf16[2048,256]{1,0:T(8,128)(2,1)S(1)} %bitcast.200, bf16[2048,256]{1,0:T(8,128)(2,1)S(1)} %bitcast.197), kind=kOutput, calls=%fused_computation.20 | convolution fusion | flops 6453460992 | bytes 14680064 | tf_op jit(solution)/shard_map/dot_general | solution.py:22
  261.0 32.0 %all-to-all-done = bf16[8,256,1024]{1,2,0:T(8,128)(2,1)} async-done(((bf16[8,256,1024]{1,2,0:T(8,128)(2,1)}), bf16[8,256,1024]{1,2,0:T(8,128)(2,1)}, u32[]{:S(2)}, u32[]{:S(2)}) %all-to-all-start) | async-done | bytes 4194336 | tf_op jit(solution)/shard_map/all_to_all | solution.py:178
  293.1 6.4 copy.64
  299.5 12.5 %fusion.40 = f32[2048,1024]{1,0:T(8,128)S(1)} fusion(bf16[2048,2048]{1,0:T(8,128)(2,1)} %all-gather.9.cloned.1.call-done, bf16[2048,1024]{1,0:T(8,128)(2,1)} %bitcast.206), kind=kOutput, calls=%fused_computation.129 | convolution fusion | flops 8589934592 | bytes 20971520 | tf_op jit(solution)/shard_map/dot_general | solution.py:22
  312.0 3.4 copy-done.25
  315.4 15.6 %convolution_convert_fusion = bf16[1024,2048]{1,0:T(8,128)(2,1)} fusion(bf16[2048,2048]{1,0:T(8,128)(2,1)} %all-gather.11.cloned.1.call-done, f32[2048,1024]{1,0:T(8,128)S(1)} %fusion.40, f32[1024]{0:T(1024)S(1)} %dynamic_slice.26), kind=kOutput, calls=%fused_computation.18 | convolution fusion | flops 8613003264 | bytes 20975616 | tf_op jit(solution)/shard_map/dot_general | solution.py:22
  331.1 19.9 %convert_reduce_fusion.3 = (f32[1024]{0:T(1024)S(1)}, bf16[2048,1024]{1,0:T(8,128)(2,1)S(1)}) fusion(f32[2048,1024]{1,0:T(8,128)} %copy-done.25, f32[1024]{0:T(1024)S(1)} %dynamic_slice.26, bf16[2048,2048]{1,0:T(8,128)(2,1)} %all-gather.11.cloned.1.call-done, bf16[1024,2048]{1,0:T(8,128)(2,1)} %param.26), kind=kOutput, calls=%fused_computation.15 | convolution fusion | flops 8636070912 | bytes 25174016 | tf_op jit(solution)/shard_map/dot_general | solution.py:22
  351.1 13.0 %convolution_convert_fusion.1 = bf16[2048,1024]{1,0:T(8,128)(2,1)S(1)} fusion(bf16[2048,2048]{1,0:T(8,128)(2,1)} %all-gather.9.cloned.1.call-done, bf16[2048,1024]{1,0:T(8,128)(2,1)S(1)} %get-tuple-element.56), kind=kOutput, calls=%fused_computation.19 | convolution fusion | flops 8592031744 | bytes 16777216 | tf_op jit(solution)/shard_map/dot_general | solution.py:22
  367.9 9.9 %fusion.35 = f32[2048,2048]{1,0:T(8,128)} fusion(bf16[2048,768]{0,1:T(8,128)(2,1)S(1)} %bitcast.210, bf16[2048,256]{1,0:T(8,128)(2,1)S(1)} %bitcast.205, bf16[2048,256]{1,0:T(8,128)(2,1)S(1)} %bitcast.201, bf16[2048,256]{1,0:T(8,128)(2,1)S(1)} %bitcast.198), kind=kOutput, calls=%fused_computation.124 | convolution fusion | flops 6451888128 | bytes 23068672 | tf_op jit(solution)/shard_map/dot_general | solution.py:22
  377.8 16.5 %add_convert_fusion = bf16[2048,2048]{1,0:T(8,128)(2,1)} fusion(f32[2048,2048]{1,0:T(8,128)} %fusion.35, bf16[2048,1024]{1,0:T(8,128)(2,1)} %copy-done.26, bf16[2048,1024]{1,0:T(8,128)(2,1)} %bitcast.207), kind=kOutput, calls=%fused_computation.2 | convolution fusion | flops 8598323200 | bytes 33554432 | tf_op jit(solution)/shard_map/dot_general | solution.py:22
  394.3 5.1 all-to-all-start.3
  401.6 91.8 %all-to-all-done.3 = bf16[8,256,2048]{2,1,0:T(8,128)(2,1)} async-done(((bf16[8,256,2048]{2,1,0:T(8,128)(2,1)}), bf16[8,256,2048]{2,1,0:T(8,128)(2,1)}, u32[]{:S(2)}, u32[]{:S(2)}) %all-to-all-start.3) | async-done | bytes 8388640 | tf_op jit(solution)/shard_map/all_to_all | solution.py:267
  493.5 4.2 all-to-all-start.4
  497.8 6.4 convert_reduce_fusion
  506.9 3.4 all-to-all-done.4
  510.9 16.8 %fusion.36 = f32[2048,2048]{1,0:T(8,128)} fusion(bf16[1024,2048]{1,0:T(8,128)(2,1)} %param.26, f32[2048,1024]{1,0:T(8,128)} %copy-done.25, f32[1024]{0:T(1024)S(1)} %dynamic_slice.26), kind=kOutput, calls=%fused_computation.125 | convolution fusion | flops 8610906112 | bytes 29364224 | tf_op jit(solution)/shard_map/dot_general | solution.py:22
  527.7 4.2 all-to-all-start.5
  531.9 11.9 %add_convert_fusion.1 = bf16[2048,2048]{1,0:T(8,128)(2,1)} fusion(f32[2048,2048]{1,0:T(8,128)} %fusion.36, bf16[2048,256]{1,0:T(8,128)(2,1)} %bitcast.189, bf16[256,2048]{1,0:T(8,128)(2,1)S(1)} %copy-done), kind=kOutput, calls=%fused_computation.4 | convolution fusion | flops 2155872256 | bytes 27262976 | tf_op jit(solution)/shard_map/dot_general | solution.py:22
  543.9 3.6 all-to-all-done.5
  547.5 5.1 all-to-all-start.2
  558.0 89.2 %all-to-all-done.2 = bf16[8,256,2048]{2,1,0:T(8,128)(2,1)} async-done(((bf16[8,256,2048]{2,1,0:T(8,128)(2,1)}), bf16[8,256,2048]{2,1,0:T(8,128)(2,1)}, u32[]{:S(2)}, u32[]{:S(2)}) %all-to-all-start.2) | async-done | bytes 8388640 | tf_op jit(solution)/shard_map/all_to_all | solution.py:267
  647.2 5.6 convert_reduce_fusion.2
  656.3 21.4 %all-reduce.2.cloned.1.call-done = f32[20480]{0:T(1024)} async-done(((f32[20480]{0:T(1024)}), f32[20480]{0:T(1024)}) %all-reduce.2.cloned.1.call-update) | async-done | bytes 81936 | tf_op jit(solution)/shard_map/psum | solution.py:303
  681.7 63.1 %all-gather.13.cloned.1.call-done = bf16[32,64,768]{2,1,0:T(8,128)(2,1)} async-done(((bf16[8,64,768]{2,1,0:T(8,128)(2,1)}), bf16[32,64,768]{2,1,0:T(8,128)(2,1)}) %all-gather.13.cloned.1.call-update) | async-done | bytes 3145744 | tf_op jit(solution)/shard_map/all_gather | solution.py:236
  744.8 10.0 %reshape.455 = f32[4,8,64,3,256]{4,3,2,1,0:T(4,128)} reshape(bf16[32,64,768]{2,1,0:T(8,128)(2,1)} %all-gather.13.cloned.1.call-done) | data formatting | bytes 9437184 | tf_op jit(solution)/shard_map/convert_element_type | solution.py:264
  754.8 9.8 %copy.70 = f32[4,64,3,8,256]{4,3,2,1,0:T(8,128)} copy(f32[4,64,3,8,256]{4,2,1,3,0:T(4,128)} %bitcast.183) | data formatting | bytes 12582912 | tf_op jit(solution)/shard_map/convert_element_type | solution.py:264
  764.6 7.5 reshape.453
  772.1 53.7 %all-gather.19.cloned.1.call-done = bf16[1024,2048]{1,0:T(8,128)(2,1)} async-done(((bf16[256,2048]{1,0:T(8,128)(2,1)}), bf16[1024,2048]{1,0:T(8,128)(2,1)}) %all-gather.19.cloned.1.call-update) | async-done | bytes 4194320 | tf_op jit(solution)/shard_map/all_gather | solution.py:236
  825.8 6.7 convert_element_type.190
  832.4 74.3 %all-gather.17.cloned.1.call-done = bf16[32,64,1024]{2,1,0:T(8,128)(2,1)} async-done(((bf16[8,64,1024]{2,1,0:T(8,128)(2,1)}), bf16[32,64,1024]{2,1,0:T(8,128)(2,1)}) %all-gather.17.cloned.1.call-update) | async-done | bytes 4194320 | tf_op jit(solution)/shard_map/all_gather | solution.py:236
  906.7 3.2 convert_bitcast_fusion
  910.0 4.9 copy.72
  914.8 11.2 %copy.82 = f32[32,8,8,1024]{3,1,2,0:T(8,128)} copy(f32[32,8,8,1024]{3,2,1,0:T(8,128)S(1)} %bitcast.185) | data formatting | bytes 16777216
  (159 shorter events, 52.5 us)
Async XLA Ops:
  7.2 103.2 %copy-start = (bf16[256,2048]{1,0:T(8,128)(2,1)S(1)}, bf16[256,2048]{1,0:T(8,128)(2,1)}, u32[]{:S(2)}) copy-start(bf16[256,2048]{1,0:T(8,128)(2,1)} %param.22) | copy-start | bytes 3145732
  7.2 103.2 %all-gather.11.cloned.1.call-start = ((), (), s32[]{:S(2)}) async-start(), calls=%async_computation.11 | async-start | bytes 9437184 | tf_op jit(solution)/shard_map/all_gather | solution.py:218
  9.2 4.7 copy-start.23
  11.7 1.0 copy-start.10
  13.9 147.9 %all-gather.9.cloned.1.call-start = ((), (), s32[]{:S(2)}) async-start(), calls=%async_computation.10 | async-start | bytes 9437184 | tf_op jit(solution)/shard_map/all_gather | solution.py:219
  30.4 9.5 %copy-start.13 = (f32[1,2,8,128]{3,1,2,0:T(2,128)}, f32[1,2,8,128]{3,1,2,0:T(2,128)S(1)}, u32[]{:S(2)}) copy-start(f32[1,2,8,128]{3,1,2,0:T(2,128)S(1)} %copy.76) | copy-start | bytes 24580
  32.3 7.6 copy-start.2
  32.3 0.6 copy-start.17
  43.8 60.2 %all-to-all-start.1 = ((bf16[8,256,3,256]{1,3,2,0:T(8,128)(2,1)}), bf16[8,256,3,256]{1,3,2,0:T(8,128)(2,1)}, u32[]{:S(2)}, u32[]{:S(2)}) async-start(bf16[8,256,3,256]{1,3,2,0:T(8,128)(2,1)} %copy.66), calls=%async_computation.1 | async-start | bytes 6291456 | tf_op jit(solution)/shard_map/all_to_all | solution.py:181
  48.3 352.9 %reduce-scatter.7.cloned.1.call-start = ((), (), s32[]{:S(2)}) async-start(), calls=%async_computation.15 | async-start | bytes 1310720 | tf_op jit(solution)/shard_map/reduce_scatter | solution.py:233
  161.9 11.8 %copy-start.1 = (f32[2,1024,128]{2,1,0:T(8,128)S(1)}, f32[2,1024,128]{2,1,0:T(8,128)}, u32[]{:S(2)}) copy-start(f32[2,1024,128]{2,1,0:T(8,128)} %get-tuple-element.32.cos_ref) | copy-start | bytes 3145732
  173.7 56.0 %copy-start.6 = (bf16[2048,2048]{1,0:T(8,128)(2,1)S(1)}, bf16[2048,2048]{1,0:T(8,128)(2,1)}, u32[]{:S(2)}) copy-start(bf16[2048,2048]{1,0:T(8,128)(2,1)} %all-gather.11.cloned.1.call-done) | copy-start | bytes 25165828
  228.7 1.0 copy-start.7
  239.4 53.7 %all-to-all-start = ((bf16[8,256,1024]{1,2,0:T(8,128)(2,1)}), bf16[8,256,1024]{1,2,0:T(8,128)(2,1)}, u32[]{:S(2)}, u32[]{:S(2)}) async-start(bf16[8,256,1024]{1,2,0:T(8,128)(2,1)} %bitcast.187), calls=%async_computation | async-start | bytes 8388608 | tf_op jit(solution)/shard_map/all_to_all | solution.py:178
  244.0 157.7 %reduce-scatter.5.cloned.1.call-start = ((), (), s32[]{:S(2)}) async-start(), calls=%async_computation.13 | async-start | bytes 3932160 | tf_op jit(solution)/shard_map/reduce_scatter | solution.py:233
  249.3 9.8 %copy-start.8 = (bf16[8,2,8,16,256]{4,3,2,1,0:T(8,128)(2,1)}, bf16[8,2,8,16,256]{4,3,2,1,0:T(8,128)(2,1)S(1)}, u32[]{:S(2)}) copy-start(bf16[8,2,8,16,256]{4,3,2,1,0:T(8,128)(2,1)S(1)} %convert_element_type.167) | copy-start | bytes 3145732
  260.9 249.5 %reduce-scatter.11.cloned.1.call-start = ((), (), s32[]{:S(2)}) async-start(), calls=%async_computation.19 | async-start | bytes 5242880 | tf_op jit(solution)/shard_map/reduce_scatter | solution.py:233
  312.0 3.4 copy-start.25
  331.0 196.7 %reduce-scatter.9.cloned.1.call-start = ((), (), s32[]{:S(2)}) async-start(), calls=%async_computation.17 | async-start | bytes 5242880 | tf_op jit(solution)/shard_map/reduce_scatter | solution.py:233
  351.0 13.1 %copy-start.26 = (bf16[2048,1024]{1,0:T(8,128)(2,1)}, bf16[2048,1024]{1,0:T(8,128)(2,1)S(1)}, u32[]{:S(2)}) copy-start(bf16[2048,1024]{1,0:T(8,128)(2,1)S(1)} %get-tuple-element.56) | copy-start | bytes 12582916
  364.1 2.6 copy-start.9
  364.1 3.7 copy-start.12
  394.3 7.3 copy-start.21
  394.3 99.2 %all-to-all-start.3 = ((bf16[8,256,2048]{2,1,0:T(8,128)(2,1)}), bf16[8,256,2048]{2,1,0:T(8,128)(2,1)}, u32[]{:S(2)}, u32[]{:S(2)}) async-start(bf16[8,256,2048]{2,1,0:T(8,128)(2,1)} %bitcast.194), calls=%async_computation.3 | async-start | bytes 16777216 | tf_op jit(solution)/shard_map/all_to_all | solution.py:267
  399.4 153.9 %all-gather.15.cloned.1.call-start = ((), (), s32[]{:S(2)}) async-start(), calls=%async_computation.16 | async-start | bytes 1310720 | tf_op jit(solution)/shard_map/all_gather | solution.py:236
  401.1 104.3 %copy-start.3 = (f32[2,128,2048]{2,1,0:T(8,128)S(1)}, f32[2,128,2048]{2,1,0:T(8,128)}, u32[]{:S(2)}) copy-start(f32[2,128,2048]{2,1,0:T(8,128)} %copy-done.2) | copy-start | bytes 6291460
  401.1 104.3 %copy-start.14 = (f32[1,2,8,128]{3,1,2,0:T(2,128)S(1)}, f32[1,2,8,128]{3,1,2,0:T(2,128)}, u32[]{:S(2)}) copy-start(f32[1,2,8,128]{3,1,2,0:T(2,128)} %copy-done.13) | copy-start | bytes 24580
  401.2 104.3 %copy-start.18 = (f32[2,128]{1,0:T(2,128)S(1)}, f32[2,128]{1,0:T(2,128)}, u32[]{:S(2)}) copy-start(f32[2,128]{1,0:T(2,128)} %copy-done.17) | copy-start | bytes 3076
  401.2 104.3 %copy-start.20 = (f32[2,128]{1,0:T(2,128)S(1)}, f32[2,128]{1,0:T(2,128)}, u32[]{:S(2)}) copy-start(f32[2,128]{1,0:T(2,128)} %get-tuple-element.33) | copy-start | bytes 3076
  493.5 16.8 %all-to-all-start.4 = ((bf16[8,64,768]{2,1,0:T(8,128)(2,1)}), bf16[8,64,768]{2,1,0:T(8,128)(2,1)}, u32[]{:S(2)}, u32[]{:S(2)}) async-start(bf16[8,64,768]{2,1,0:T(8,128)(2,1)} %reduce-scatter.5.cloned.1.call-done), calls=%async_computation.5 | async-start | bytes 1572864 | tf_op jit(solution)/shard_map/all_to_all | solution.py:242
  497.7 180.0 %all-reduce.2.cloned.1.call-start = ((), (), s32[]{:S(2)}) async-start(), calls=%async_computation.12 | async-start | bytes 163840 | tf_op jit(solution)/shard_map/psum | solution.py:303
  504.1 1.3 copy-start.4
  506.2 0.6 copy-start.15
  506.9 237.9 %all-gather.13.cloned.1.call-start = ((), (), s32[]{:S(2)}) async-start(), calls=%async_computation.14 | async-start | bytes 3932160 | tf_op jit(solution)/shard_map/all_gather | solution.py:236
  510.3 315.4 %all-gather.19.cloned.1.call-start = ((), (), s32[]{:S(2)}) async-start(), calls=%async_computation.20 | async-start | bytes 5242880 | tf_op jit(solution)/shard_map/all_gather | solution.py:236
  527.7 19.8 %all-to-all-start.5 = ((bf16[8,64,1024]{2,1,0:T(8,128)(2,1)}), bf16[8,64,1024]{2,1,0:T(8,128)(2,1)}, u32[]{:S(2)}, u32[]{:S(2)}) async-start(bf16[8,64,1024]{2,1,0:T(8,128)(2,1)} %reduce-scatter.9.cloned.1.call-done), calls=%async_computation.8 | async-start | bytes 2097152 | tf_op jit(solution)/shard_map/all_to_all | solution.py:242
  547.5 5.8 copy-start.16
  547.5 99.7 %all-to-all-start.2 = ((bf16[8,256,2048]{2,1,0:T(8,128)(2,1)}), bf16[8,256,2048]{2,1,0:T(8,128)(2,1)}, u32[]{:S(2)}, u32[]{:S(2)}) async-start(bf16[8,256,2048]{2,1,0:T(8,128)(2,1)} %bitcast.184), calls=%async_computation.2 | async-start | bytes 16777216 | tf_op jit(solution)/shard_map/all_to_all | solution.py:267
  552.6 354.2 %all-gather.17.cloned.1.call-start = ((), (), s32[]{:S(2)}) async-start(), calls=%async_computation.18 | async-start | bytes 5242880 | tf_op jit(solution)/shard_map/all_gather | solution.py:236
  556.1 96.6 %copy-start.19 = (s32[1,1,2,128]{3,2,1,0:T(2,128)S(1)}, s32[1,1,2,128]{3,2,1,0:T(2,128)}, u32[]{:S(2)}) copy-start(s32[1,1,2,128]{3,2,1,0:T(2,128)} %param.16) | copy-start | bytes 3076
  556.1 96.6 %copy-start.24 = (pred[2,128]{1,0:T(4,128)(4,1)S(1)}, pred[2,128]{1,0:T(4,128)(4,1)}, u32[]{:S(2)}) copy-start(pred[2,128]{1,0:T(4,128)(4,1)} %copy-done.23) | copy-start | bytes 772
  647.1 7.1 copy-start.5
  647.1 7.1 copy-start.11
  679.0 247.0 %copy-start.22 = (f32[256]{0:T(256)}, f32[256]{0:T(256)S(1)}, u32[]{:S(2)}) copy-start(f32[256]{0:T(256)S(1)} %get-tuple-element.84) | copy-start | bytes 3076
Sparse Core Ops, SparseCore 0:
  14.1 82.4 all-gather.10
  99.0 62.8 all-gather.8
  233.1 27.1 reduce-scatter.6
  262.6 60.0 reduce-scatter.4
  331.2 75.9 reduce-scatter.10
  409.3 77.2 reduce-scatter.8
  488.2 28.4 all-gather.14
  523.8 153.8 all-reduce.1
  679.3 65.4 all-gather.12
  746.3 79.3 all-gather.18
  827.4 79.2 all-gather.16

commit v2 on v1

--- a/solution.py
+++ b/solution.py
@@ -1,8 +1,8 @@
-import functools
 import math
 
 import jax
 import jax.numpy as jnp
+import numpy as np
 from jax import lax
 from jax.experimental import pallas as pl
 from jax.experimental.pallas import tpu as pltpu
@@ -16,6 +16,7 @@
 MAXBLK = 8
 PAIR = 2 * HDIM
 NEG = -1e30
+FUSED_BYTES = 48 << 20
 
 
 def dot(left, right, dims, out=jnp.float32):
@@ -31,7 +32,19 @@
     return begins, limits
 
 
-def attention_kernel(begin_ref, q_ref, k_ref, v_ref, do_ref, cos_ref, low_ref, high_ref, kid_ref,
+def rotary_tables():
+    half = ROT // 2
+    lane = np.arange(PAIR) % HDIM
+    freqs = np.exp(-math.log(10000.0) * np.arange(half) * 2.0 / ROT).astype(np.float32)
+    position = np.arange(MAXBLK * BLOCK, dtype=np.float32)
+    angles = (position[:, None] * freqs[lane % half][None, :]).astype(np.float64)
+    sines = np.sin(angles)
+    cosine = np.where(lane < ROT, np.cos(angles), 1.0)
+    signed = np.where(lane < half, -sines, np.where(lane < ROT, sines, 0.0))
+    return [jnp.asarray(t.astype(np.float32)) for t in (cosine, signed)]
+
+
+def attention_kernel(begin_ref, q_ref, k_ref, v_ref, do_ref, cos_ref, sin_ref, kid_ref,
                      ob_ref, dq_ref, dk_ref, dv_ref, ks, vs, dks, dvs):
     micro = pl.program_id(0)
     blocks = q_ref.shape[1]
@@ -42,15 +55,14 @@
         return ref[:, j].reshape(BLOCK, PAIR)
 
     def table(ref, j):
-        return ref[j * BLOCK:(j + 1) * BLOCK, :]
+        return ref[pl.ds(pl.multiple_of((j - begin_ref[micro, j]) * BLOCK, BLOCK), BLOCK), :]
 
     def turn(x, j, back):
-        up = pltpu.roll(x, PAIR - half, 1)
-        down = pltpu.roll(x, half, 1)
-        low, high = table(low_ref, j), table(high_ref, j)
-        if back:
-            return x * table(cos_ref, j) - up * low - down * high
-        return x * table(cos_ref, j) + up * low + down * high
+        other = jnp.where(
+            lane % HDIM < half, pltpu.roll(x, PAIR - half, 1), pltpu.roll(x, half, 1)
+        ) * table(sin_ref, j)
+        straight = x * table(cos_ref, j)
+        return straight - other if back else straight + other
 
     for j in range(blocks):
         ks[j * BLOCK:(j + 1) * BLOCK, :] = turn(rows(k_ref, j), j, False).astype(jnp.bfloat16)
@@ -108,7 +120,7 @@
         dv_ref[:, j] = dvs[here, :].astype(jnp.bfloat16).astype(jnp.float32).reshape(shape)
 
 
-def attention(begins, qkv, dout, cosine, low, high, kid):
+def attention(begins, qkv, dout, kid):
     group, micros, blocks, cap, _ = qkv.shape
     width = dout.shape[-1]
     pairs = width // PAIR
@@ -119,7 +131,7 @@
             (group, None, blocks, cap, PAIR), lambda m, p, *_: (0, m, 0, 0, offset + p)
         )
 
-    table_spec = pl.BlockSpec((None, total, PAIR), lambda m, p, *_: (m, 0, 0))
+    table_spec = pl.BlockSpec((MAXBLK * BLOCK, PAIR), lambda m, p, *_: (0, 0))
     out = jax.ShapeDtypeStruct(dout.shape, jnp.float32)
     work = micros * pairs * 2 * blocks * (min(blocks, MAXBLK) + 1) // 2 * BLOCK * BLOCK
     return pl.pallas_call(
@@ -129,7 +141,7 @@
             grid=(micros, pairs),
             in_specs=[
                 rows_spec(0), rows_spec(pairs), rows_spec(2 * pairs), rows_spec(0),
-                table_spec, table_spec, table_spec,
+                table_spec, table_spec,
                 pl.BlockSpec((None, 1, total), lambda m, p, *_: (m, 0, 0)),
             ],
             out_specs=[rows_spec(0)] * 4,
@@ -145,7 +157,737 @@
         cost_estimate=pl.CostEstimate(
             flops=12 * work * PAIR, bytes_accessed=8 * dout.size * 4, transcendentals=work
         ),
-    )(begins, qkv, qkv, qkv, dout, cosine, low, high, kid)
+    )(begins, qkv, qkv, qkv, dout, *rotary_tables(), kid)
+
+
+MESH = pl.DeviceIdType.MESH
+SLOTS = 4
+TILES = 4
+
+
+def fused_kernel(
+    begin_ref, kid_ref, bq_ref, bf_ref, tables, gy_home, hn_home, fc1_w, qkv_w, fc2_w, dense_w,
+    grad, grad_a, grad_b, grad_t, gq, gq_a, gq_b, gq_t, part_in, home, vec_f, vec_q,
+    gy, hn, fc1, fc2, wqkv, dense, act, dup, ob, dqkv, qkv, dout, ks, vs, dks, dvs, tt, gst, ast,
+    pb, vb, table,
+    load, ag_send, ag_recv, w_send, w_recv, st, g_send, g_own, g_recv, za_s, za_r, zb_s, zb_r, zc_s,
+    zc_r, zt, zl, d_send, p_recv, h_recv,
+):
+    bf16, f32 = jnp.bfloat16, jnp.float32
+    me, rep = lax.axis_index("shard"), lax.axis_index("rep")
+    core, cx, cy = me % 2, (me // 2) % 2, me // 4
+    near = rep + 1 - 2 * (rep % 2)
+    far = 3 - rep
+    inner = (rep == 1) | (rep == 2)
+    outer = (rep == 0) | (rep == 3)
+    rows_home = gy_home.shape[0]
+    width = gy_home.shape[1]
+    ff = fc1.shape[1]
+    tile = ff // TILES
+    wide = 512
+    pairs = wqkv.shape[0]
+    cols3 = 3 * PAIR
+
+    def flip(e):
+        return ((cy + e // 4) % 2) * 4 + ((cx + (e // 2) % 2) % 2) * 2 + (core + e % 2) % 2
+
+    def at_shard(d):
+        return {"shard": d}
+
+    def at_rep(d):
+        return {"rep": d}
+
+    def remote(src, dst, send, recv, dev):
+        return pltpu.make_async_remote_copy(
+            src_ref=src, dst_ref=dst, send_sem=send, recv_sem=recv, device_id=dev,
+            device_id_type=MESH,
+        )
+
+    def local(src, dst, sem):
+        return pltpu.make_async_copy(src, dst, sem)
+
+    def span(i, size):
+        return pl.ds(pl.multiple_of(i * size, size), size)
+
+    def own(ref, q):
+        return ref.at[span(q, rows_home), :]
+
+    loads = [
+        local(gy_home, own(gy, me), load.at[0]),
+        local(hn_home, own(hn, me), load.at[1]),
+        local(fc2_w, fc2, load.at[2]),
+        local(dense_w, dense, load.at[3]),
+        local(fc1_w.at[:, span(me, ff)], own(fc1, me), load.at[4]),
+        local(qkv_w.at[me], wqkv.at[:, span(me, rows_home), :], load.at[5]),
+    ]
+    for copy in loads:
+        copy.start()
+
+    barrier = pltpu.get_barrier_semaphore()
+    for e in range(1, 8):
+        pl.semaphore_signal(barrier, inc=1, device_id=at_shard(flip(e)), device_id_type=MESH)
+    pl.semaphore_signal(barrier, inc=1, device_id=at_rep(near), device_id_type=MESH)
+    pl.semaphore_signal(barrier, inc=1, device_id=at_rep(far), device_id_type=MESH)
+    pl.semaphore_wait(barrier, 9)
+
+    pairs_in = ((gy_home, gy), (hn_home, hn))
+    for a, (source, buf) in enumerate(pairs_in):
+        for n, e in enumerate((2, 4, 1)):
+            remote(source, own(buf, me), ag_send.at[a, n], ag_recv.at[a, e], at_shard(flip(e))).start()
+
+    def send_fc1(i):
+        for e in range(1, 8):
+            d = flip(e)
+            remote(
+                fc1_w.at[:, pl.ds(pl.multiple_of(d * ff + i * tile, tile), tile)],
+                fc1.at[span(me, rows_home), pl.ds(i * tile, tile)],
+                w_send.at[0], w_recv.at[i], at_shard(d),
+            ).start()
+
+    def ag_wait(a, e):
+        buf = pairs_in[a][1]
+        remote(own(buf, me), own(buf, flip(e)), ag_send.at[a, 0], ag_recv.at[a, e],
+               at_shard(flip(e))).wait_recv()
+
+    def forward(a, have, to, n):
+        buf = pairs_in[a][1]
+        q = own(buf, flip(have))
+        remote(q, q, ag_send.at[a, n], ag_recv.at[a, have ^ to], at_shard(flip(to))).start()
+
+    send_fc1(0)
+    for a in range(2):
+        ag_wait(a, 2)
+        forward(a, 2, 1, 4)
+
+        @pl.when(core == 0)
+        def _():
+            forward(a, 2, 4, 3)
+
+        ag_wait(a, 4)
+        forward(a, 4, 1, 5)
+
+        @pl.when(core == 1)
+        def _():
+            forward(a, 4, 2, 3)
+
+    for i in range(1, TILES):
+        send_fc1(i)
+    for e in range(1, 8):
+        d = flip(e)
+        remote(qkv_w.at[d], wqkv.at[:, span(me, rows_home), :], w_send.at[1], w_recv.at[TILES],
+               at_shard(d)).start()
+    for copy in loads:
+        copy.wait()
+    for a in range(2):
+        ag_wait(a, 6)
+        forward(a, 6, 1, 6)
+    for a in range(2):
+        for e in (1, 3, 5, 7):
+            ag_wait(a, e)
+
+    uniform = 2 * grad.shape[0]
+    half = rows_home // 2
+    units = uniform + 2 * pairs
+
+    def unit(u):
+        if isinstance(u, int) and u >= uniform:
+            v = u - uniform
+            where = (v // 2, pl.ds((v % 2) * half, half), slice(None))
+            return [ref.at[where] for ref in (gq, gq_a, gq_b, gq_t)] + [gq.shape[2]]
+        where = (u // 2, pl.ds(pl.multiple_of((u % 2) * half, half), half), slice(None))
+        return [ref.at[where] for ref in (grad, grad_a, grad_b, grad_t)] + [width]
+
+    def chain_a(u):
+        g, a, _, _, _ = unit(u)
+
+        @pl.when(outer)
+        def _():
+            remote(g, a, za_s.at[u], za_r.at[u], at_rep(near)).start()
+
+    def chain_b(u):
+        g, a, b, t, n = unit(u)
+        slot = u % SLOTS
+        mine = pb.at[slot, :, 0:n]
+
+        @pl.when(inner)
+        def _():
+            remote(g, a, za_s.at[u], za_r.at[u], at_rep(near)).wait_recv()
+            two = local(a, vb.at[:, 0:n], zl.at[1])
+            two.start()
+
+            def clear():
+                old = unit(u - SLOTS)
+                past = pb.at[slot, :, 0:old[4]]
+                remote(past, old[3], zc_s.at[u - SLOTS], zc_r.at[u - SLOTS], at_rep(near)).wait_send()
+                local(past, old[3], zt.at[u - SLOTS]).wait()
+
+            if not isinstance(u, int) or u >= SLOTS:
+                clear()
+            one = local(g, mine, zl.at[0])
+            one.start()
+            one.wait()
+            two.wait()
+            pb[slot, :, 0:n] = (
+                pb[slot, :, 0:n].astype(f32) + vb[:, 0:n].astype(f32)
+            ).astype(bf16)
+            remote(mine, b, zb_s.at[u], zb_r.at[u], at_rep(far)).start()
+
+    def chain_c(u):
+        g, a, b, t, n = unit(u)
+        slot = u % SLOTS
+        mine = pb.at[slot, :, 0:n]
+
+        @pl.when(inner)
+        def _():
+            remote(mine, b, zb_s.at[u], zb_r.at[u], at_rep(far)).wait()
+            two = local(b, vb.at[:, 0:n], zl.at[1])
+            two.start()
+            two.wait()
+            pb[slot, :, 0:n] = (
+                pb[slot, :, 0:n].astype(f32) + vb[:, 0:n].astype(f32)
+            ).astype(bf16)
+            remote(mine, t, zc_s.at[u], zc_r.at[u], at_rep(near)).start()
+            local(mine, t, zt.at[u]).start()
+
+    done = [0]
+
+    def advance(count=1):
+        for _ in range(count):
+            u = done[0]
+            if u < units:
+                chain_b(u)
+            if 0 < u <= units:
+                chain_c(u - 1)
+            done[0] = u + 1
+
+    scale_in = math.sqrt(2.0 / math.pi)
+
+    def hidden(i):
+        cols = slice(i * tile, (i + 1) * tile)
+        bias = bf_ref[:, cols]
+
+        def step(rb, total):
+            rows = span(rb, rows_home)
+            u = dot(hn[rows, :], fc1[:, cols], ((1,), (0,))) + bias
+            d = dot(gy[rows, :], fc2[cols, :], ((1,), (1,)))
+            square = u * u
+            t = jnp.tanh(scale_in * u * (1.0 + 0.044715 * square))
+            a = 0.5 * u * (1.0 + t)
+            slope = 0.5 * (1.0 + t) + 0.5 * u * (1.0 - t * t) * scale_in * (
+                1.0 + 3 * 0.044715 * square
+            )
+            d = d * slope
+            act[rows, cols] = a.astype(bf16)
+            tt[0:tile, rows] = a.T.astype(bf16)
+            low = d.astype(bf16)
+            dup[rows, cols] = low
+            tt[tile:2 * tile, rows] = d.T.astype(bf16)
+            return total + jnp.sum(low.astype(f32), axis=0, keepdims=True)
+
+        vec_f[:, cols] = lax.fori_loop(0, width // rows_home, step, jnp.zeros((1, tile), f32))
+
+    def grad_fc2(i, slot):
+        def step(cb, _):
+            cols = span(cb, wide)
+            gst[slot, :, cols] = dot(tt[0:tile, :], gy[:, cols], ((1,), (0,))).astype(bf16)
+            return 0
+
+        lax.fori_loop(0, width // wide, step, 0)
+        local(gst.at[slot], grad.at[2 * i], st.at[slot]).start()
+
+    def spread(slot, n, place, index):
+        local(ast.at[slot, me, :, 0:n], place(me), g_own.at[slot]).start()
+        for e in range(1, 8):
+            d = flip(e)
+            remote(ast.at[slot, d, :, 0:n], place(me), g_send.at[slot], g_recv.at[index],
+                   at_shard(d)).start()
+
+    def spread_sent(slot, n):
+        block = ast.at[slot, 0:7, :, 0:n]
+        local(block, block, g_send.at[slot]).wait()
+
+    def spread_here(slot, n, place, block, index):
+        local(ast.at[slot, me, :, 0:n], place(me), g_own.at[slot]).wait()
+        local(block, block, g_recv.at[index]).wait()
+
+    def fc1_place(i):
+        return lambda q: grad.at[2 * i + 1, :, span(q, tile)]
+
+    def grad_fc1(i, slot):
+        if i >= 2:
+            spread_sent(slot, tile)
+
+        def step(db, _):
+            g = dot(tt[tile:2 * tile, :], hn[:, span(db, rows_home)], ((1,), (0,)))
+            ast[slot, db, :, 0:tile] = g.T.astype(bf16)
+            return 0
+
+        lax.fori_loop(0, width // rows_home, step, 0)
+        spread(slot, tile, fc1_place(i), i)
+
+    def fc1_here(i):
+        spread_here(i % 2, tile, fc1_place(i), grad.at[2 * i + 1, :, 0:7 * tile], i)
+        chain_a(4 * i + 2)
+        chain_a(4 * i + 3)
+
+    for i in range(TILES):
+        block = fc1.at[0:7 * rows_home, pl.ds(i * tile, tile)]
+        local(block, block, w_recv.at[i]).wait()
+        hidden(i)
+        if i:
+            fc1_here(i - 1)
+        if i >= 2:
+            advance()
+        grad_fc2(i, i % 2)
+        grad_fc1(i, i % 2)
+        local(gst.at[i % 2], grad.at[2 * i], st.at[i % 2]).wait()
+        chain_a(4 * i)
+        chain_a(4 * i + 1)
+        if i:
+            advance()
+    block = wqkv.at[:, 0:7 * rows_home, :]
+    local(block, block, w_recv.at[TILES]).wait()
+
+    blocks = kid_ref.shape[2] // BLOCK
+    packs = kid_ref.shape[0]
+    cap = qkv.shape[3]
+    scale = 1.0 / math.sqrt(HDIM)
+    turn_by = ROT // 2
+    lane = lax.broadcasted_iota(jnp.int32, (BLOCK, PAIR), 1)
+    causal = lax.broadcasted_iota(jnp.int32, (BLOCK, BLOCK), 1) <= lax.broadcasted_iota(
+        jnp.int32, (BLOCK, BLOCK), 0
+    )
+    zero = jnp.zeros((), bf16)
+
+    def attend(it, first_unit):
+        p, m = it // packs, it % packs
+        fetch = local(tables.at[m], table, load.at[0])
+        fetch.start()
+
+        @pl.when(m == 0)
+        def _():
+            def project(sb, _):
+                rows = span(sb, rows_home)
+                r = dot(hn[rows, :], wqkv[p], ((1,), (0,))) + bq_ref[p]
+                qkv[sb] = r.reshape(packs, blocks, cap, cols3)
+                d = dot(gy[rows, :], dense[p], ((1,), (1,)))
+                dout[sb] = d.astype(bf16).reshape(packs, blocks, cap, PAIR)
+                return 0
+
+            lax.fori_loop(0, width // rows_home, project, 0)
+            vec_q[p] = jnp.zeros((1, cols3), f32)
+
+        chain_b(first_unit)
+        chain_c(first_unit - 1)
+        fetch.wait()
+
+        def rows_of(which, j):
+            return qkv[:, m, j, :, which * PAIR:(which + 1) * PAIR].reshape(BLOCK, PAIR)
+
+        def turn(x, j, back):
+            here = slice(j * BLOCK, (j + 1) * BLOCK)
+            other = jnp.where(
+                lane % HDIM < turn_by, pltpu.roll(x, PAIR - turn_by, 1), pltpu.roll(x, turn_by, 1)
+            ) * table[1, here, :]
+            straight = x * table[0, here, :]
+            return straight - other if back else straight + other
+
+        for j in range(blocks):
+            ks[j * BLOCK:(j + 1) * BLOCK, :] = turn(rows_of(1, j), j, False).astype(bf16)
+            vs[j * BLOCK:(j + 1) * BLOCK, :] = rows_of(2, j).astype(bf16)
+        dks[...] = jnp.zeros_like(dks)
+        dvs[...] = jnp.zeros_like(dvs)
+        first_head = lane < HDIM
+
+        def put(ref, j, lanes, value):
+            ref[p, :, m, j, :, lanes] = value.astype(bf16).reshape(width // rows_home, cap, PAIR)
+
+        total_q = jnp.zeros((1, PAIR), f32)
+        for j in range(blocks):
+            first = max(0, j - MAXBLK + 1)
+            keys_at = slice(first * BLOCK, (j + 1) * BLOCK)
+            q_all = turn(rows_of(0, j), j, False).astype(bf16)
+            do_all = dout[:, m, j, :, :].reshape(BLOCK, PAIR)
+            keys, values = ks[keys_at, :], vs[keys_at, :]
+            bias = jnp.where(kid_ref[m, :, keys_at] == begin_ref[m, j], 0.0, NEG)
+            long = (j - first) * BLOCK
+            outs, dqs = [], []
+            for head in range(PAIR // HDIM):
+                mine = first_head if head == 0 else jnp.logical_not(first_head)
+                q = jnp.where(mine, q_all, zero)
+                do = jnp.where(mine, do_all, zero)
+                scores = dot(q, keys, ((1,), (1,))) * scale + bias
+                tail = jnp.where(causal, scores[:, long:], NEG)
+                scores = jnp.concatenate([scores[:, :long], tail], axis=1) if long else tail
+                top = jnp.max(scores, axis=1, keepdims=True)
+                expo = jnp.exp(scores - top)
+                probs = expo * (1.0 / jnp.sum(expo, axis=1, keepdims=True))
+                low_probs = probs.astype(bf16)
+                outs.append(dot(low_probs, values, ((1,), (0,))))
+                dprobs = dot(do, values, ((1,), (1,)))
+                weighted = probs * dprobs
+                delta = jnp.sum(weighted, axis=1, keepdims=True)
+                dscores = (weighted - probs * delta).astype(bf16)
+                dqs.append(dot(dscores, keys, ((1,), (0,))))
+                dks[keys_at, :] += dot(dscores, q, ((0,), (0,)))
+                dvs[keys_at, :] += dot(low_probs, do, ((0,), (0,)))
+            put(ob, j, slice(0, PAIR), jnp.where(first_head, outs[0], outs[1]))
+            dq = turn(jnp.where(first_head, dqs[0], dqs[1]) * scale, j, True)
+            put(dqkv, j, slice(0, PAIR), dq)
+            total_q += jnp.sum(dq.astype(bf16).astype(f32), axis=0, keepdims=True)
+        total_k = jnp.zeros((1, PAIR), f32)
+        total_v = jnp.zeros((1, PAIR), f32)
+        for j in range(blocks):
+            here = slice(j * BLOCK, (j + 1) * BLOCK)
+            dk = turn(dks[here, :] * scale, j, True)
+            dv = dvs[here, :]
+            put(dqkv, j, slice(PAIR, 2 * PAIR), dk)
+            put(dqkv, j, slice(2 * PAIR, 3 * PAIR), dv)
+            total_k += jnp.sum(dk.astype(bf16).astype(f32), axis=0, keepdims=True)
+            total_v += jnp.sum(dv.astype(bf16).astype(f32), axis=0, keepdims=True)
+        vec_q[p] += jnp.concatenate([total_q, total_k, total_v], axis=1)
+        chain_b(first_unit + 1)
+        chain_c(first_unit)
+
+    fc1_here(TILES - 1)
+    start = done[0]
+
+    def attend_step(it, _):
+        attend(it, start + 2 * it)
+        return 0
+
+    lax.fori_loop(0, pairs * packs, attend_step, 0)
+    done[0] = start + 2 * pairs * packs
+
+    def qkv_place(p):
+        return lambda q: gq.at[p, :, pl.ds(pl.multiple_of(q * cols3, PAIR), cols3)]
+
+    dense_chunk = grad.shape[0] - 1
+    for p in range(pairs):
+        def turn_round(sb, _):
+            cols = span(sb, rows_home)
+            t = dqkv[p, sb].reshape(rows_home, cols3).astype(f32)
+            tt[0:cols3, cols] = t.T.astype(bf16)
+            o = ob[p, sb].reshape(rows_home, PAIR).astype(f32)
+            tt[cols3:cols3 + PAIR, cols] = o.T.astype(bf16)
+            return 0
+
+        lax.fori_loop(0, width // rows_home, turn_round, 0)
+
+        def step(cb, _):
+            cols = span(cb, wide)
+            gst[0, pl.ds(p * PAIR, PAIR), cols] = dot(
+                tt[cols3:cols3 + PAIR, :], gy[:, cols], ((1,), (0,))
+            ).astype(bf16)
+            return 0
+
+        lax.fori_loop(0, width // wide, step, 0)
+        spread_sent(p % 2, tile)
+
+        def step_qkv(db, _):
+            g = dot(tt[0:cols3, :], hn[:, span(db, rows_home)], ((1,), (0,)))
+            ast[p % 2, db, :, :] = g.T.astype(bf16)
+            return 0
+
+        lax.fori_loop(0, width // rows_home, step_qkv, 0)
+        spread(p % 2, cols3, qkv_place(p), TILES + p)
+        advance()
+    local(gst.at[0], grad.at[dense_chunk], st.at[0]).start()
+    local(gst.at[0], grad.at[dense_chunk], st.at[0]).wait()
+    chain_a(2 * dense_chunk)
+    chain_a(2 * dense_chunk + 1)
+    for p in range(pairs):
+        spread_here(p % 2, cols3, qkv_place(p), gq.at[p, :, 0:7 * cols3], TILES + p)
+        chain_a(uniform + 2 * p)
+        chain_a(uniform + 2 * p + 1)
+
+    def part(which, q, cols):
+        rows = span(q, rows_home)
+        if which == 0:
+            acc = dot(act[rows, :], fc2[:, cols], ((1,), (0,)))
+            for p in range(pairs):
+                acc += dot(ob[p, q].reshape(rows_home, PAIR), dense[p, :, cols], ((1,), (0,)))
+            return acc
+        acc = dot(dup[rows, :], fc1[cols, :], ((1,), (1,)))
+        for p in range(pairs):
+            acc += dot(dqkv[p, q].reshape(rows_home, cols3), wqkv[p, cols, :], ((1,), (1,)))
+        return acc
+
+    chips = part_in.shape[1]
+    for which in range(2):
+        def give(c, _):
+            slot = c % 2
+
+            @pl.when(c >= 2)
+            def _():
+                local(gst.at[slot], gst.at[slot], d_send.at[slot]).wait()
+
+            def step(cb, _):
+                cols = span(cb, wide)
+                gst[slot, :, cols] = part(which, 2 * c + 1 - core, cols).astype(bf16)
+                return 0
+
+            lax.fori_loop(0, width // wide, step, 0)
+            remote(gst.at[slot], part_in.at[which, c], d_send.at[slot],
+                   p_recv.at[which * chips + c], at_shard(flip(1))).start()
+            return 0
+
+        lax.fori_loop(0, chips, give, 0)
+        for slot in range(2):
+            local(gst.at[slot], gst.at[slot], d_send.at[slot]).wait()
+        advance()
+
+    partner = tt.at[0:rows_home, :]
+    for which in range(2):
+        def chip_of(c):
+            return ((cy + c // 2) % 2) * 2 + (cx + c % 2) % 2
+
+        def total(c, slot):
+            chip = chip_of(c)
+            remote(gst.at[slot], part_in.at[which, chip], d_send.at[slot],
+                   p_recv.at[which * chips + chip], at_shard(flip(1))).wait_recv()
+            copy = local(part_in.at[which, chip], partner, load.at[0])
+            copy.start()
+            copy.wait()
+
+            def step(cb, _):
+                cols = span(cb, wide)
+                gst[slot, :, cols] = (
+                    part(which, 2 * chip + core, cols) + tt[0:rows_home, cols].astype(f32)
+                ).astype(bf16)
+                return 0
+
+            lax.fori_loop(0, width // wide, step, 0)
+
+        def keep(c, _):
+            slot = c % 2
+
+            @pl.when(c >= 3)
+            def _():
+                local(gst.at[slot], gst.at[slot], d_send.at[slot]).wait()
+
+            total(c, slot)
+            remote(gst.at[slot], home.at[which, c], d_send.at[slot],
+                   h_recv.at[which * chips + c], at_shard(2 * chip_of(c) + core)).start()
+            return 0
+
+        lax.fori_loop(1, chips, keep, 0)
+        local(gst.at[0], gst.at[0], d_send.at[0]).wait()
+        total(0, 0)
+        local(gst.at[0], home.at[which, 0], st.at[0]).start()
+        local(gst.at[0], home.at[which, 0], st.at[0]).wait()
+        local(gst.at[1], gst.at[1], d_send.at[1]).wait()
+        advance()
+
+    while done[0] <= units:
+        advance()
+
+    @pl.when(outer)
+    def _():
+        for u in range(units):
+            g, a, b, t, _ = unit(u)
+            remote(g, a, za_s.at[u], za_r.at[u], at_rep(near)).wait_send()
+            remote(g, t, zc_s.at[u], zc_r.at[u], at_rep(near)).wait_recv()
+
+    @pl.when(inner)
+    def _():
+        for u in range(units - SLOTS, units):
+            g, a, b, t, n = unit(u)
+            past = pb.at[u % SLOTS, :, 0:n]
+            remote(past, t, zc_s.at[u], zc_r.at[u], at_rep(near)).wait_send()
+            local(past, t, zt.at[u]).wait()
+
+    for a in range(2):
+        for n in range(7):
+            buf = pairs_in[a][1]
+            remote(own(buf, me), own(buf, me), ag_send.at[a, n], ag_recv.at[a, 1],
+                   at_shard(flip(1))).wait_send()
+    block = fc1.at[0:7 * rows_home, :]
+    local(block, block, w_send.at[0]).wait()
+    block = wqkv.at[:, 0:7 * rows_home, :]
+    local(block, block, w_send.at[1]).wait()
+    for p in range(pairs):
+        spread_sent(p % 2, cols3)
+    for which in range(2):
+        for c in range(1, chips):
+            remote(gst.at[0], home.at[which, c], d_send.at[0], h_recv.at[which * chips + c],
+                   at_shard(flip(2))).wait_recv()
+
+
+def fused(begins, key_id, bq, bf, turns, gy_home, hn_home, fc1_w, qkv_w, fc2_w, dense_w, group):
+    bf16, f32 = jnp.bfloat16, jnp.float32
+    rows, width = gy_home.shape
+    ff = fc1_w.shape[1] // group
+    tile = ff // TILES
+    pairs = dense_w.shape[0]
+    packs, blocks = begins.shape
+    cap = rows // packs // blocks
+    total = group * rows
+    chips = group // 2
+    units = 2 * (2 * TILES + 1) + 2 * pairs
+    chunk = jax.ShapeDtypeStruct((2 * TILES + 1, rows, width), bf16)
+    chunk_q = jax.ShapeDtypeStruct((pairs, rows, group * 3 * PAIR), bf16)
+    parts = jax.ShapeDtypeStruct((2, chips, rows, width), bf16)
+    out_shape = [chunk] * 4 + [chunk_q] * 4 + [parts] * 2 + [
+        jax.ShapeDtypeStruct((1, ff), f32), jax.ShapeDtypeStruct((pairs, 1, 3 * PAIR), f32)
+    ]
+    vmem = pl.BlockSpec(memory_space=pltpu.VMEM)
+    anywhere = pl.BlockSpec(memory_space=pl.ANY)
+    dma = pltpu.SemaphoreType.DMA
+    per = (group, packs, blocks, cap)
+    pack_rows = blocks * BLOCK
+    scratch = [
+        pltpu.VMEM((total, width), bf16), pltpu.VMEM((total, width), bf16),
+        pltpu.VMEM((width, ff), bf16), pltpu.VMEM((ff, width), bf16),
+        pltpu.VMEM((pairs, width, 3 * PAIR), bf16), pltpu.VMEM((pairs, PAIR, width), bf16),
+        pltpu.VMEM((total, ff), bf16), pltpu.VMEM((total, ff), bf16),
+        pltpu.VMEM((pairs,) + per + (PAIR,), bf16), pltpu.VMEM((pairs,) + per + (3 * PAIR,), bf16),
+        pltpu.VMEM(per + (3 * PAIR,), f32), pltpu.VMEM(per + (PAIR,), bf16),
+        pltpu.VMEM((pack_rows, PAIR), bf16), pltpu.VMEM((pack_rows, PAIR), bf16),
+        pltpu.VMEM((pack_rows, PAIR), f32), pltpu.VMEM((pack_rows, PAIR), f32),
+        pltpu.VMEM((2 * tile, total), bf16),
+        pltpu.VMEM((2, rows, width), bf16), pltpu.VMEM((2, group, rows, 3 * PAIR), bf16),
+        pltpu.VMEM((SLOTS, rows // 2, group * 3 * PAIR), bf16),
+        pltpu.VMEM((rows // 2, group * 3 * PAIR), bf16),
+        pltpu.VMEM((2, pack_rows, PAIR), f32),
+        dma((6,)), dma((2, 7)), dma((2, 8)), dma((2,)), dma((TILES + 1,)), dma((2,)), dma((2,)),
+        dma((2,)), dma((TILES + pairs,)),
+        dma((units,)), dma((units,)), dma((units,)), dma((units,)), dma((units,)), dma((units,)),
+        dma((units,)), dma((2,)), dma((2,)), dma((2 * chips,)), dma((2 * chips,)),
+    ]
+    flops = 6 * total * (2 * width * ff + width * pairs * 4 * PAIR)
+    return pl.pallas_call(
+        fused_kernel,
+        in_specs=[pl.BlockSpec(memory_space=pltpu.SMEM)] + [vmem] * 3 + [anywhere] * 7,
+        out_specs=[anywhere] * 10 + [vmem] * 2,
+        out_shape=out_shape,
+        scratch_shapes=scratch,
+        compiler_params=pltpu.CompilerParams(
+            vmem_limit_bytes=60 << 20, collective_id=0, has_side_effects=True
+        ),
+        cost_estimate=pl.CostEstimate(
+            flops=flops, bytes_accessed=64 << 20, transcendentals=total * ff
+        ),
+    )(begins, key_id, bq, bf, turns, gy_home, hn_home, fc1_w, qkv_w, fc2_w, dense_w)
+
+
+def spread_layer(
+    gy_home, hn_home, begins, key_id, qkv_weight, b_qkv, dense_weight, fc1_weight, b_fc1, fc2_weight
+):
+    bf16, f32 = jnp.bfloat16, jnp.float32
+    group, reps = lax.axis_size("shard"), lax.axis_size("rep")
+    width = gy_home.shape[1]
+    rows = gy_home.shape[0] // MICRO
+    cap = rows // group
+    mine = width // group
+    ff_mine = fc1_weight.shape[1] // group
+    blocks = begins.shape[1]
+    all_rows = MICRO * rows * group
+
+    fc1 = lax.all_to_all(
+        fc1_weight.reshape(mine, group, ff_mine).transpose(1, 0, 2), "shard", 0, 0, tiled=True
+    ).reshape(width, ff_mine)
+    w_qkv = lax.all_to_all(
+        qkv_weight.reshape(mine, 3, group, mine).transpose(2, 0, 1, 3), "shard", 0, 0, tiled=True
+    ).reshape(width, 3 * mine)
+
+    gy = lax.all_gather(gy_home, "shard", axis=0, tiled=True)
+    hn = lax.all_gather(hn_home, "shard", axis=0, tiled=True)
+
+    upper = dot(hn, fc1, ((1,), (0,))) + b_fc1
+    inner = math.sqrt(2.0 / math.pi) * (upper + 0.044715 * upper * upper * upper)
+    curve = jnp.tanh(inner)
+    act = (0.5 * upper * (1.0 + curve)).astype(bf16)
+    slope = 0.5 * (1.0 + curve) + 0.5 * upper * (1.0 - curve * curve) * math.sqrt(
+        2.0 / math.pi
+    ) * (1.0 + 3 * 0.044715 * upper * upper)
+    dup = (dot(gy, fc2_weight, ((1,), (1,))) * slope).astype(bf16)
+    g_fc2 = dot(act, gy, ((0,), (0,)), f32).astype(bf16)
+    g_fc1 = dot(hn, dup, ((0,), (0,)), f32).astype(bf16)
+
+    def over_reps(part):
+        return lax.psum_scatter(part, "rep", scatter_dimension=0, tiled=True)
+
+    def from_reps(part):
+        return lax.all_gather(part, "rep", axis=0, tiled=True)
+
+    def by_rows(grad):
+        cols = grad.shape[1]
+        split = grad.reshape(group, reps, mine // reps, cols).transpose(1, 0, 2, 3)
+        part = over_reps(split.reshape(reps * group, mine // reps, cols))
+        part = lax.all_to_all(part, "shard", 0, 0, tiled=True)
+        whole = from_reps(part)
+        return whole.reshape(reps, group, mine // reps, cols)
+
+    grad_fc2 = from_reps(over_reps(g_fc2)).astype(f32)
+    grad_fc1 = by_rows(g_fc1).transpose(0, 2, 1, 3).reshape(mine, -1).astype(f32)
+
+    qkv = dot(hn, w_qkv, ((1,), (0,))) + b_qkv
+    dout = dot(gy, dense_weight, ((1,), (1,)))
+    shape = (group, MICRO, blocks, cap)
+    ob, dq, dk, dv = attention(
+        begins, qkv.reshape(*shape, 3 * mine), dout.reshape(*shape, mine), key_id
+    )
+    ob = ob.reshape(all_rows, mine).astype(bf16)
+    dqkv = jnp.concatenate(
+        [part.reshape(all_rows, mine).astype(bf16) for part in (dq, dk, dv)], axis=1
+    )
+    g_qkv = dot(hn, dqkv, ((0,), (0,)), f32).astype(bf16)
+    g_dense = dot(ob, gy, ((0,), (0,)), f32).astype(bf16)
+    grad_dense = from_reps(over_reps(g_dense)).astype(f32)
+    grad_qkv = by_rows(g_qkv).reshape(reps, group, mine // reps, 3, mine)
+    grad_qkv = grad_qkv.transpose(0, 2, 3, 1, 4).reshape(mine, 3 * width).astype(f32)
+
+    def home(part):
+        got = lax.all_to_all(part.reshape(group, MICRO * rows, width), "shard", 0, 0, tiled=True)
+        return jnp.sum(got.astype(f32), axis=0)
+
+    out_part = (
+        dot(act, fc2_weight, ((1,), (0,))) + dot(ob, dense_weight, ((1,), (0,)))
+    ).astype(bf16)
+    dh_part = (dot(dqkv, w_qkv, ((1,), (1,))) + dot(dup, fc1, ((1,), (1,)))).astype(bf16)
+    v_qkv = jnp.sum(dqkv.astype(f32), axis=0).reshape(3, mine)
+    v_fc1 = jnp.sum(dup.astype(f32), axis=0)
+    return (
+        home(out_part), home(dh_part), grad_qkv, grad_dense, grad_fc1, grad_fc2, v_qkv, v_fc1
+    )
+
+
+def fused_layer(
+    gy_home, hn_home, begins, key_id, qkv_weight, b_qkv, dense_weight, fc1_weight, b_fc1, fc2_weight
+):
+    f32 = jnp.float32
+    group = lax.axis_size("shard")
+    width = gy_home.shape[1]
+    mine = width // group
+    pairs = mine // PAIR
+    ff_mine = fc1_weight.shape[1] // group
+    tile = ff_mine // TILES
+    qkv_w = qkv_weight.reshape(mine, 3, group, pairs, PAIR).transpose(2, 3, 0, 1, 4)
+    bq = b_qkv.reshape(3, pairs, PAIR).transpose(1, 0, 2).reshape(pairs, 1, 3 * PAIR)
+    blocks = begins.shape[1]
+    index = jnp.arange(blocks, dtype=jnp.int32)
+    offset = index[None, :] - begins
+    pick = (offset[:, :, None] == jnp.arange(MAXBLK, dtype=jnp.int32)[None, None, :]).astype(f32)
+    turns = jnp.einsum(
+        "mjo,tox->mtjx", pick, jnp.stack(rotary_tables()).reshape(2, MAXBLK, BLOCK * PAIR),
+        precision=lax.Precision.HIGHEST,
+    ).reshape(begins.shape[0], 2, blocks * BLOCK, PAIR)
+    outs = fused(
+        begins, key_id, bq, b_fc1.reshape(1, ff_mine), turns, gy_home, hn_home, fc1_weight,
+        qkv_w.reshape(group, pairs, mine, 3 * PAIR), fc2_weight,
+        dense_weight.reshape(pairs, PAIR, width), group,
+    )
+    grad_t, gq_t, home, vec_f, vec_q = outs[3], outs[7], outs[9], outs[10], outs[11]
+    grad_fc2 = grad_t[0:2 * TILES:2].reshape(ff_mine, width).astype(f32)
+    grad_fc1 = grad_t[1:2 * TILES:2].reshape(TILES, mine, group, tile).transpose(1, 2, 0, 3)
+    grad_fc1 = grad_fc1.reshape(mine, group * ff_mine).astype(f32)
+    grad_dense = grad_t[2 * TILES].astype(f32)
+    grad_qkv = gq_t.reshape(pairs, mine, group, 3, PAIR).transpose(1, 3, 2, 0, 4)
+    grad_qkv = grad_qkv.reshape(mine, 3 * width).astype(f32)
+    v_qkv = vec_q.reshape(pairs, 3, PAIR).transpose(1, 0, 2).reshape(3, mine)
+    sums = jnp.sum(home.astype(f32), axis=1)
+    return sums[0], sums[1], grad_qkv, grad_dense, grad_fc1, grad_fc2, v_qkv, vec_f.reshape(-1)
 
 
 def body(
@@ -175,27 +917,12 @@
     b_qkv = lax.dynamic_slice_in_dim(b_qkv.reshape(3, width), me * mine, mine, 1).reshape(-1)
     b_fc1 = lax.dynamic_slice_in_dim(b_fc1, me * ff_mine, ff_mine, 0)
 
-    fc1 = lax.all_to_all(
-        fc1_weight.reshape(mine, group, ff_mine).transpose(1, 0, 2), "shard", 0, 0, tiled=True
-    ).reshape(width, ff_mine)
-    w_qkv = lax.all_to_all(
-        qkv_weight.reshape(mine, 3, group, mine).transpose(2, 0, 1, 3), "shard", 0, 0, tiled=True
-    ).reshape(width, 3 * mine)
-
     begins, limits = block_begins(seq_lengths[0])
     spot = jnp.arange(BLOCK, dtype=jnp.int32)
     index = jnp.arange(blocks, dtype=jnp.int32)
     position = (index[None, :, None] - begins[:, :, None]) * BLOCK + spot[None, None, :]
     valid = position < limits[:, :, None]
     key_id = jnp.where(valid, begins[:, :, None], -1).reshape(MICRO, 1, blocks * BLOCK)
-    lane = jnp.arange(PAIR, dtype=jnp.int32) % HDIM
-    half = ROT // 2
-    freqs = jnp.exp(-math.log(10000.0) * jnp.arange(half, dtype=f32) * 2.0 / ROT)
-    angles = position.reshape(MICRO, -1, 1).astype(f32) * freqs[lane % half]
-    sines = jnp.sin(angles)
-    cosine = jnp.where(lane < ROT, jnp.cos(angles), 1.0)
-    low = jnp.where(lane < half, -sines, 0.0)
-    high = jnp.where((lane >= half) & (lane < ROT), sines, 0.0)
 
     orders = placement_order[0, 0]
     select = (orders[:, None, :] == jnp.arange(rows, dtype=jnp.int32)[None, :, None]).astype(bf16)
@@ -215,65 +942,19 @@
     centered = x32 - jnp.mean(x32, axis=1, keepdims=True)
     rstd = lax.rsqrt(jnp.mean(centered * centered, axis=1, keepdims=True) + 1e-05)
     hn_home = (centered * rstd * gain + lnb).astype(bf16)
-    gy = lax.all_gather(gy_home, "shard", axis=0, tiled=True)
-    hn = lax.all_gather(hn_home, "shard", axis=0, tiled=True)
-
-    upper = dot(hn, fc1, ((1,), (0,))) + b_fc1
-    inner = math.sqrt(2.0 / math.pi) * (upper + 0.044715 * upper * upper * upper)
-    curve = jnp.tanh(inner)
-    act = (0.5 * upper * (1.0 + curve)).astype(bf16)
-    slope = 0.5 * (1.0 + curve) + 0.5 * upper * (1.0 - curve * curve) * math.sqrt(
-        2.0 / math.pi
-    ) * (1.0 + 3 * 0.044715 * upper * upper)
-    dup = (dot(gy, fc2_weight, ((1,), (1,))) * slope).astype(bf16)
-    g_fc2 = dot(act, gy, ((0,), (0,)), f32).astype(bf16)
-    g_fc1 = dot(hn, dup, ((0,), (0,)), f32).astype(bf16)
-
-    def over_reps(part):
-        return lax.psum_scatter(part, "rep", scatter_dimension=0, tiled=True)
-
-    def from_reps(part):
-        return lax.all_gather(part, "rep", axis=0, tiled=True)
-
-    def by_rows(grad):
-        cols = grad.shape[1]
-        split = grad.reshape(group, reps, mine // reps, cols).transpose(1, 0, 2, 3)
-        part = over_reps(split.reshape(reps * group, mine // reps, cols))
-        part = lax.all_to_all(part, "shard", 0, 0, tiled=True)
-        whole = from_reps(part)
-        return whole.reshape(reps, group, mine // reps, cols)
-
-    grad_fc2 = from_reps(over_reps(g_fc2)).astype(f32)
-    grad_fc1 = by_rows(g_fc1).transpose(0, 2, 1, 3).reshape(mine, -1).astype(f32)
-
-    qkv = dot(hn, w_qkv, ((1,), (0,))) + b_qkv
-    dout = dot(gy, dense_weight, ((1,), (1,)))
-    shape = (group, MICRO, blocks, cap)
-    ob, dq, dk, dv = attention(
-        begins, qkv.reshape(*shape, 3 * mine), dout.reshape(*shape, mine), cosine, low, high,
-        key_id,
+    split = (
+        gy_home, hn_home, begins, key_id, qkv_weight, b_qkv, dense_weight, fc1_weight, b_fc1,
+        fc2_weight,
     )
-    ob = ob.reshape(all_rows, mine).astype(bf16)
-    dqkv = jnp.concatenate(
-        [part.reshape(all_rows, mine).astype(bf16) for part in (dq, dk, dv)], axis=1
-    )
-    g_qkv = dot(hn, dqkv, ((0,), (0,)), f32).astype(bf16)
-    g_dense = dot(ob, gy, ((0,), (0,)), f32).astype(bf16)
-    grad_dense = from_reps(over_reps(g_dense)).astype(f32)
-    grad_qkv = by_rows(g_qkv).reshape(reps, group, mine // reps, 3, mine)
-    grad_qkv = grad_qkv.transpose(0, 2, 3, 1, 4).reshape(mine, 3 * width).astype(f32)
-
-    def home(part):
-        got = lax.all_to_all(part.reshape(group, MICRO * rows, width), "shard", 0, 0, tiled=True)
-        return jnp.sum(got.astype(f32), axis=0)
-
-    out_part = (
-        dot(act, fc2_weight, ((1,), (0,))) + dot(ob, dense_weight, ((1,), (0,)))
-    ).astype(bf16)
-    dh_part = (dot(dqkv, w_qkv, ((1,), (1,))) + dot(dup, fc1, ((1,), (1,)))).astype(bf16)
-    branch = home(out_part) + (b_dense + b_fc2)
+    held = 2 * MICRO * rows * group * (2 * width + 2 * ff_mine + 7 * mine)
+    held += 2 * width * (2 * ff_mine + 4 * mine)
+    if (group, reps) == (8, 4) and cap % 16 == 0 and held <= FUSED_BYTES:
+        result = fused_layer(*split)
+    else:
+        result = spread_layer(*split)
+    out_sum, dh, grad_qkv, grad_dense, grad_fc1, grad_fc2, v_qkv, v_fc1 = result
+    branch = out_sum + (b_dense + b_fc2)
     mixed = (x32 + jnp.where(valid_home, branch, 0.0)).astype(bf16)
-    dh = home(dh_part)
     xhat = centered * rstd
     scaled = dh * gain
     dx = (
@@ -289,24 +970,18 @@
             preferred_element_type=f32,
         ).astype(bf16).reshape(MICRO * rows, width)
 
-    def placed(part, count, offset):
-        return lax.dynamic_update_slice_in_dim(
-            jnp.zeros((count,) + part.shape[1:], f32), part, offset, 0
-        )
-
-    v_qkv = jnp.sum(dqkv.astype(f32), axis=0).reshape(3, mine).T
-    v_qkv = placed(v_qkv, width, me * mine).T.reshape(-1)
-    v_fc1 = placed(jnp.sum(dup.astype(f32), axis=0), group * ff_mine, me * ff_mine)
     v_out = jnp.sum(gy_home.astype(f32), axis=0)
     v_gain = jnp.sum(dh * xhat, axis=0)
     v_lnb = jnp.sum(dh, axis=0)
-    sums = lax.psum(jnp.concatenate([v_qkv, v_fc1, v_out, v_gain, v_lnb]), ("rep", "shard"))
-    outs, at = [], 0
-    for count in (3 * width, group * ff_mine, width, width, width):
-        share = count // group
-        outs.append(lax.dynamic_slice_in_dim(sums, at + me * share, share, 0))
-        at += count
-    bias_qkv, bias_fc1, bias_out, gain_grad, lnb_grad = outs
+    mixed_vec = jnp.concatenate([v_qkv.reshape(-1), v_fc1, v_out, v_gain, v_lnb])
+    table = lax.all_gather(mixed_vec, ("rep", "shard"), axis=0).reshape(reps, group, -1)
+    table = jnp.sum(table, axis=0)
+    at = 3 * mine
+    bias_qkv = table[:, :at].reshape(group, 3, mine).transpose(1, 0, 2).reshape(-1)
+    bias_qkv = lax.dynamic_slice_in_dim(bias_qkv, me * 3 * mine, 3 * mine, 0)
+    bias_fc1 = lax.dynamic_index_in_dim(table[:, at:at + ff_mine], me, 0, keepdims=False)
+    full = jnp.sum(table[:, at + ff_mine:], axis=0).reshape(3, group, mine)
+    bias_out, gain_grad, lnb_grad = lax.dynamic_index_in_dim(full, me, 1, keepdims=False)
     return (
         back(mixed), back(token_grad), gain_grad, lnb_grad, grad_qkv, bias_qkv, grad_dense,
         bias_out, grad_fc1, bias_fc1, grad_fc2, bias_out,

time: 940 us -> 795 us (0.85)
  Pallas kernels: 54.9 us -> 612 us
  waiting for transfers between devices: 518 us -> 0 us
  matrix products: 156 us -> 12 us
  blocking collectives: 10.7 us -> 54 us
  starting transfers between devices: 28.3 us -> 0 us
  other arithmetic: 55.3 us -> 30.4 us
  local copies, waits for them, and re-layouts: 95.9 us -> 74.3 us
  between operations: 14.8 us -> 1.3 us
    pallas_call x1, Pallas kernels: 54.9 us -> 612 us  [fused(): pl.pallas_call(fused_kernel, in_specs=[pl.BlockSpec(memory_space=pltpu.SM...]
    all_to_all x6 -> x0, waiting for transfers between devices: 259 us -> none  [the longest x2 181 us: home(): lax.all_to_all(part.reshape(group, MICRO * rows, width), 'shard', 0, 0, t...]
    all_gather x6 -> x0, waiting for transfers between devices: 235 us -> none  [the longest x4 191 us: from_reps(): return lax.all_gather(part, 'rep', axis=0, tiled=True)]
    dot_general x12 -> x1, matrix products: 148 us -> 3.57 us  [fused_layer(): jnp.einsum('mjo,tox->mtjx', pick, jnp.stack(rotary_tables()).reshape(2, M...]
    all_gather x0 -> x1, blocking collectives: none -> 43.3 us  [body(): lax.all_gather(mixed_vec, ('rep', 'shard'), axis=0).reshape(reps, group, -1)]
    all_to_all x6 -> x0, starting transfers between devices: 27.7 us -> none  [the longest x2 10.2 us: home(): lax.all_to_all(part.reshape(group, MICRO * rows, width), 'shard', 0, 0, t...]
    psum x1 -> x0, waiting for transfers between devices: 21.4 us -> none  [body(): lax.psum(jnp.concatenate([v_qkv, v_fc1, v_out, v_gain, v_lnb]), ('rep', '...]
    unnamed x76 -> x46, local copies, waits for them, and re-layouts: 39 us -> 17.9 us
  transfers between devices with their start and end apart: 17 -> 0, of which waited for: 11 -> 0; matrix products, arithmetic and copies ran while one was open for 28% -> 0% of each run, Pallas kernels for 0% -> 0%
where the time goes in v2:
time: 795 us; the launch traced here: 784 us
  Pallas kernels  612 us (77%)
  local copies, waits for them, and re-layouts  74.3 us (9%)
  blocking collectives  54 us (7%)
  other arithmetic  30.4 us (4%)
  matrix products  12 us (2%)
    pallas_call x1, Pallas kernels, fused(): pl.pallas_call(fused_kernel, in_specs=[pl.BlockSpec(memory_space=pltpu.SM...  612 us
    all_gather x1, blocking collectives, body(): lax.all_gather(mixed_vec, ('rep', 'shard'), axis=0).reshape(reps, group, -1)  43.3 us
    convert_element_type x3, local copies, waits for them, and re-layouts, fused_layer(): grad_fc1 = grad_fc1.reshape(mine, group * ff_mine).astype(f32)  26.8 us
    unnamed x46, local copies, waits for them, and re-layouts  17.9 us

profile of v2, /device:TPU:0, one launch (start us, length us, event | category | flops | bytes accessed | tf_op | source)
XLA Modules:
  0.0 783.6 jit_solution(8672065956931768246)
XLA Ops:
  0.7 0.8 broadcast_compare_fusion
  1.5 0.1 select_reduce_fusion.1.begin_ref
  1.6 0.9 select_reduce_fusion
  2.6 0.1 broadcast_in_dim.93
  2.7 1.3 convert_reduce_fusion.1
  4.1 1.2 bitcast_select_fusion.gy_home
  5.3 1.9 fusion.24
  7.2 0.4 multiply_reduce_fusion.1
  7.6 0.2 dynamic-update-slice.5
  7.9 0.2 dynamic-update-slice.6
  8.1 0.2 dynamic-update-slice.7
  8.3 0.2 dynamic-update-slice.8
  8.5 0.2 dynamic-update-slice.9
  8.8 0.2 dynamic-update-slice.10
  9.0 10.7 %all-gather.2 = bf16[8,1,2816]{2,1,0:T(2,128)(2,1)S(1)} all-gather(bf16[1,1,2816]{2,1,0:T(2,128)(2,1)S(1)} %reshape.352), channel_id=2, replica_groups=mesh['rep'=4,'shard'=8] {'shard'}, dimensions={0}, use_global_device_ids=true | all-gather | bytes 50688 | tf_op jit(solution)/shard_map/all_gather | solution.py:911
  19.7 1.4 add_convert_fusion.2.hn_home
  21.2 0.6 dynamic_slice.23
  21.8 0.6 reshape.361.bq_ref
  22.6 0.6 compare_select_fusion.kid_ref
  23.3 3.6 convolution_bitcast_fusion
  26.8 2.7 reshape.362
  29.5 3.0 copy.81.tables
  32.6 4.6 copy.69
  37.2 3.9 copy.70
  41.1 4.6 copy.72.qkv_w
  45.7 611.6 %shard_map.247 = (bf16[9,256,2048]{2,1,0:T(8,128)(2,1)}, bf16[9,256,2048]{2,1,0:T(8,128)(2,1)}, bf16[9,256,2048]{2,1,0:T(8,128)(2,1)}, bf16[9,256,2048]{2,1,0:T(...) custom-call(s32[2,8]{1,0:T(2,128)} %copy-done.3, ...), custom_call_target="tpu_custom_call" | custom-call | flops 77309411328 | bytes 67108864 | tf_op jit(solution)/shard_map/pallas_call | solution.py:759
  657.4 0.7 reduce.4
  658.1 0.7 constant_dynamic-update-slice_fusion.3
  658.8 5.7 convert_reduce_fusion
  664.5 0.8 fusion.1
  665.4 2.3 slice_reduce_fusion.1
  667.7 43.3 %all-gather.3 = f32[32,1,7936]{2,1,0:T(1,128)S(1)} all-gather(f32[1,1,7936]{2,1,0:T(1,128)S(1)} %reshape.354), channel_id=3, replica_groups=mesh['rep'=4,'shard'=8] {'rep','shard'}, dimensions={0}, use_global_device_ids=true | all-gather | bytes 1047552 | tf_op jit(solution)/shard_map/all_gather | solution.py:977
  711.1 0.7 dynamic_slice.25
  711.9 0.6 constant_dynamic-slice_fusion.3
  712.5 0.6 constant_dynamic-slice_fusion.2
  713.1 3.7 convolution_convert_fusion
  716.8 1.5 convolution_convert_fusion.1
  718.3 5.8 fusion.23
  724.1 4.1 copy.90
  728.3 4.0 bitcast_bitcast_fusion
  732.3 12.1 %copy.76 = f32[256,8,4,256]{3,2,1,0:T(4,128)} copy(f32[256,8,4,256]{3,1,0,2:T(8,128)} %bitcast_bitcast_fusion) | data formatting | bytes 16777216 | tf_op jit(solution)/shard_map/convert_element_type | solution.py:884
  744.4 10.7 %reshape.344 = f32[256,8192]{1,0:T(8,128)} reshape(f32[256,8,4,256]{3,2,1,0:T(4,128)} %copy.76) | data formatting | bytes 16777216 | tf_op jit(solution)/shard_map/convert_element_type | solution.py:884
  755.1 6.7 bitcast_convert_fusion
  761.7 2.8 bitcast_convert_fusion.1
  764.5 5.4 copy.74
  769.9 6.2 copy.75
  776.1 6.6 copy.77
  782.7 0.6 copy.109
  (64 shorter events, 0.8 us)
Async XLA Ops:
  0.6 2.0 copy-start
  1.6 21.0 %copy-start.3 = (s32[2,8]{1,0:T(2,128)}, s32[2,8]{1,0:T(2,128)S(1)}, u32[]{:S(2)}) copy-start(s32[2,8]{1,0:T(2,128)S(1)} %select_reduce_fusion.1.begin_ref) | copy-start | bytes 196
  2.7 2.6 copy-start.4
  5.3 2.3 copy-start.8
  5.3 2.6 copy-start.9
  5.3 2.8 copy-start.10
  5.3 3.0 copy-start.11
  5.3 3.2 copy-start.6
  5.3 3.4 copy-start.7
  712.5 70.2 %copy-start.5 = (f32[1,1,256]{2,1,0:T(1,128)}, f32[1,1,256]{2,1,0:T(1,128)S(1)}, u32[]{:S(2)}) copy-start(f32[1,1,256]{2,1,0:T(1,128)S(1)} %get-tuple-element.69) | copy-start | bytes 3076
  713.1 3.7 copy-start.2
  776.0 7.2 copy-start.1
